TPU v7x, 256 devices: a whole 4x4x8 slice. The times are simulated.
256 devices in a mesh: row: 16 (over x, z_hi), col: 16 (over y, z_lo, core).
Axes of the slice: x: 4, y: 4, z: 8 (z_hi: 4, z_lo: 2; z = z_hi * 2 + z_lo), core: 2. Of those that a mesh axis runs over, the one named last changes fastest.
Arguments:
- tile_count: int32 [16, 16], P('row', 'col'), may hold values from 1 to 40, as said below
- tile_rows: int32 [16, 16, 40], P('row', 'col'), may hold values from 0 to 31, as said below
- tile_cols: int32 [16, 16, 40], P('row', 'col'), may hold values from 0 to 31, as said below
- tiles: float32 [16, 16, 40, 256, 256], P('row', 'col')
- block: float32 [64, 131072], P(None, ('row', 'col')), may hold values from -6 to 6
Outputs:
- image_x: float32 [64, 131072], P(None, ('row', 'col'))
- image_w: float32 [64, 131072], P(None, ('row', 'col'))
- grams: float32 [4, 64, 64], replicated
Inputs may be any that keep to these rules, and one draw needn't show every extreme that they name: `tile_count`: live slots of each grid block; the largest count over the grid is exactly 40. `tile_rows`: live slots of one grid block hold distinct positions whose global tile row is at least the global tile column; slots at or past the count hold 0. `tile_cols`: paired with tile_rows as above; slots at or past the count hold 0.
All inputs are finite; a program needn't handle non-finite values.
Results may differ from a plain program's by a relative error of at most 0.0001.
Values sent between devices are 32-bit elements; how exact they have to be, the bound alone decides.
A program may use at most 64 MiB of HBM per device.

v0:
```python
import jax
import jax.numpy as jnp
from jax import lax
from jax.sharding import PartitionSpec as P

highest = lax.Precision.HIGHEST


def passed_along(array, axis, by):
    size = lax.axis_size(axis)
    return lax.ppermute(array, axis, [(i, (i + by) % size) for i in range(size)])


def inner_prod(left, right):
    return lax.dot_general(
        left, right, (((1,), (1,)), ((), ())), precision=highest, preferred_element_type=jnp.float32
    )


def on_device(tile_count, tile_rows, tile_cols, tiles, block):
    vec_count, seg_rows = block.shape
    tile_size = tiles.shape[-1]
    seg_tiles = seg_rows // tile_size
    grid_rows = lax.axis_size("row")
    grid_cols = lax.axis_size("col")
    total_rows = seg_rows * grid_rows * grid_cols
    live_count = tile_count[0, 0]
    row_ids = tile_rows[0, 0]
    col_ids = tile_cols[0, 0]
    tile_data = tiles[0, 0]
    row_slots = grid_cols * seg_tiles
    col_slots = grid_rows * seg_tiles

    def expand(vectors):
        near_vec = lax.all_gather(vectors, "col", axis=1, tiled=True)
        far_vec = lax.all_gather(vectors, "row", axis=1, tiled=True)
        near_tiles = near_vec.reshape(vec_count, row_slots, tile_size)
        far_tiles = far_vec.reshape(vec_count, col_slots, tile_size)
        groups = (live_count + 7) // 8

        def accumulate(counter, carry):
            sums_rows, sums_cols = carry
            offset = counter * 8
            block_tiles = lax.dynamic_slice_in_dim(tile_data, offset, 8, 0)
            slot_rows = lax.dynamic_slice_in_dim(row_ids, offset, 8, 0)
            slot_cols = lax.dynamic_slice_in_dim(col_ids, offset, 8, 0)
            live_mask = (offset + jnp.arange(8, dtype=jnp.int32) < live_count).astype(jnp.float32)
            rows_in = jnp.take(near_tiles, slot_rows, axis=1)
            cols_in = jnp.take(far_tiles, slot_cols, axis=1)
            lower_part = (
                jnp.einsum("sij,ksj->ksi", block_tiles, cols_in, precision=highest)
                * live_mask[None, :, None]
            )
            upper_part = (
                jnp.einsum("sij,ksi->ksj", block_tiles, rows_in, precision=highest)
                * live_mask[None, :, None]
            )
            row_pick = (
                slot_rows[:, None] == jnp.arange(row_slots, dtype=jnp.int32)[None, :]
            ).astype(jnp.float32)
            col_pick = (
                slot_cols[:, None] == jnp.arange(col_slots, dtype=jnp.int32)[None, :]
            ).astype(jnp.float32)
            sums_rows = sums_rows + jnp.einsum(
                "ksi,sp->kpi", lower_part, row_pick, precision=highest
            )
            sums_cols = sums_cols + jnp.einsum(
                "ksi,sp->kpi", upper_part, col_pick, precision=highest
            )
            return (sums_rows, sums_cols)

        empty_rows = jnp.zeros((vec_count, row_slots, tile_size), jnp.float32)
        empty_cols = jnp.zeros((vec_count, col_slots, tile_size), jnp.float32)
        part_rows, part_cols = lax.fori_loop(0, groups, accumulate, (empty_rows, empty_cols))
        return (
            near_vec,
            far_vec,
            part_rows.reshape(vec_count, row_slots * tile_size),
            part_cols.reshape(vec_count, col_slots * tile_size),
        )

    def combine_sums(part_rows, part_cols):
        pieces_rows = part_rows.reshape(vec_count, grid_cols, seg_rows)
        pieces_cols = part_cols.reshape(vec_count, grid_rows, seg_rows)
        my_col = lax.axis_index("col")
        my_row = lax.axis_index("row")

        def select_piece(pieces, position):
            return lax.dynamic_index_in_dim(pieces, position, 1, keepdims=False)

        def pass_along_rows(counter, running):
            moved = passed_along(running, "col", 1)
            return moved + select_piece(
                pieces_rows, (my_col + 2 * grid_cols - 1 - counter) % grid_cols
            )

        def pass_along_cols(counter, running):
            moved = passed_along(running, "row", 1)
            return moved + select_piece(
                pieces_cols, (my_row + 2 * grid_rows - 1 - counter) % grid_rows
            )

        first_rows = select_piece(pieces_rows, (my_col + grid_cols - 1) % grid_cols)
        first_cols = select_piece(pieces_cols, (my_row + grid_rows - 1) % grid_rows)
        own_rows = lax.fori_loop(1, grid_cols, pass_along_rows, first_rows)
        own_cols = lax.fori_loop(1, grid_rows, pass_along_cols, first_cols)
        return own_rows + own_cols

    near_x, far_x, rows_x, cols_x = expand(block)
    image_x = combine_sums(rows_x, cols_x)
    first_term = inner_prod(block, image_x)
    rayleigh = lax.psum(first_term, ("row", "col")) / total_rows
    resid = image_x - jnp.dot(
        rayleigh, block, precision=highest, preferred_element_type=jnp.float32
    )
    near_w, far_w, rows_w, cols_w = expand(resid)
    image_w = combine_sums(rows_w, cols_w)
    cross_term = inner_prod(block, image_w)
    resid_term = inner_prod(resid, image_w)
    square_term = inner_prod(resid, resid)
    others = lax.psum(jnp.stack([cross_term, resid_term, square_term]), ("row", "col")) / total_rows
    grams = jnp.concatenate([rayleigh[None], others], axis=0)
    return (image_x, image_w, grams)


def solution(mesh):
    return jax.shard_map(
        on_device,
        mesh=mesh,
        in_specs=(
            P("row", "col"),
            P("row", "col", None),
            P("row", "col", None),
            P("row", "col", None, None, None),
            P(None, ("row", "col")),
        ),
        out_specs=(P(None, ("row", "col")), P(None, ("row", "col")), P()),
        check_vma=False,
    )
```

profile of v0, /device:TPU:1, one launch (start us, length us, event | category | flops | bytes accessed | tf_op | source)
XLA Modules:
  0.0 1058.2 jit_solution(5392531176664811493)
XLA Ops:
  9.4 40.8 %all-gather.7.cloned.1.call-done = f32[64,8192]{1,0:T(8,128)} async-done(((f32[64,512]{1,0:T(8,128)}), f32[64,8192]{1,0:T(8,128)}) %all-gather.7.cloned.1.call-update) | async-done | bytes 2097168 | tf_op jit(solution)/shard_map/all_gather | solution.py:35
  53.4 56.9 %all-gather.5.cloned.1.call-done = f32[64,8192]{1,0:T(8,128)} async-done(((f32[64,512]{1,0:T(8,128)}), f32[64,8192]{1,0:T(8,128)}) %all-gather.5.cloned.1.call-update) | async-done | bytes 2097168 | tf_op jit(solution)/shard_map/all_gather | solution.py:36
  115.4 17.8 %while.84 = (s32[]{:T(128)}, f32[64,32,256]{2,1,0:T(8,128)S(1)}, f32[64,32,256]{2,1,0:T(8,128)}, s32[]{:T(128)}, s32[40]{0:T(128)S(1)}, /*index=5*/s32[40]{0:T(1...) while((s32[]{:T(128)}, f32[64,32,256]{2,1,0:T(8,128)S(1)}, ...), condition=%wide.region_1.3_spmd, body=%wide.region_0.2_spmd.sunk | while | flops 907545280 | bytes 17834760 | solution.py:74
  140.4 203.6 %while.86 = (s32[]{:T(128)}, f32[64,512]{1,0:T(8,128)S(1)}, s32[]{:T(128)}, f32[64,16,512]{2,1,0:T(8,128)}, s32[]{:T(128)}, /*index=5*/s32[]{:T(128)}, s32[]{:T(128)}, s32[]{:T(128)}) while((s32[]{:T(128)}, f32[64,512]{1,0:T(8,128)S(1)}, s32[]{:T(128)}, f32[64,16,512]{2,1,0:T(8,128)}, s32[]{:T(128)}, /*index=5*/s32[]{:T(128)}, s32[]{:T(128)}, ...), condition=%wide.region_5.7_spmd, body=%wide.region_4.6_spmd.sunk | while | flops 32785 | bytes 1179932 | solution.py:106
  143.3 75.8 %collective-permute-done.1 = f32[64,512]{1,0:T(8,128)S(1)} collective-permute-done((f32[64,512]{1,0:T(8,128)S(1)}, f32[64,512]{1,0:T(8,128)S(1)}, u32[]{:S(2)}, u32[]{:S(2)}) %collective-permute-start.1) | collective-permute-done | bytes 131104 | tf_op jit(solution)/shard_map/while/body/eval_jaxpr/ppermute | solution.py:11
  220.6 6.7 collective-permute-done.1
  228.7 6.7 collective-permute-done.1
  236.9 6.7 collective-permute-done.1
  245.1 7.9 collective-permute-done.1
  254.5 7.8 collective-permute-done.1
  263.8 6.7 collective-permute-done.1
  271.9 7.4 collective-permute-done.1
  280.8 7.6 collective-permute-done.1
  289.9 7.5 collective-permute-done.1
  298.8 6.7 collective-permute-done.1
  307.0 6.8 collective-permute-done.1
  315.2 6.8 collective-permute-done.1
  323.5 8.6 collective-permute-done.1
  333.6 10.4 collective-permute-done.1
  344.0 115.5 %while.85 = (s32[]{:T(128)}, f32[64,512]{1,0:T(8,128)S(1)}, s32[]{:T(128)}, f32[64,16,512]{2,1,0:T(8,128)}, s32[]{:T(128)}, /*index=5*/s32[]{:T(128)}, s32[]{:T(128)}, s32[]{:T(128)}) while((s32[]{:T(128)}, f32[64,512]{1,0:T(8,128)S(1)}, s32[]{:T(128)}, f32[64,16,512]{2,1,0:T(8,128)}, s32[]{:T(128)}, /*index=5*/s32[]{:T(128)}, s32[]{:T(128)}, ...), condition=%wide.region_3.5_spmd, body=%wide.region_2.4_spmd.sunk | while | flops 32785 | bytes 1179932 | solution.py:105
  344.0 23.9 %collective-permute-start = (f32[64,512]{1,0:T(8,128)S(1)}, f32[64,512]{1,0:T(8,128)S(1)}, u32[]{:S(2)}, u32[]{:S(2)}) collective-permute-start(f32[64,512]{1,0:T(8,128)S(1)} %get-tuple-element.1026), channel_id=1, source_target_pairs={{0,1},{1,2},{2,3},{3,4},{4,5},{5,6},{6,7},{7,8},{8,9},{9,10},{10,1... | collective-permute-start | bytes 393224 | tf_op jit(solution)/shard_map/while/body/eval_jaxpr/ppermute | solution.py:11
  408.1 5.1 collective-permute-done
  414.7 5.1 collective-permute-done
  421.3 5.1 collective-permute-done
  459.9 76.2 %psum.14 = f32[64,64]{0,1:T(8,128)S(1)} all-reduce(f32[64,64]{0,1:T(8,128)S(1)} %convolution_bitcast_fusion.3), channel_id=1, replica_groups=mesh['row'=16,'col'=16] {'row','col'}, use_global_device_ids=true, to_apply=%region_6.8 | all-reduce | flops 4096 | bytes 32768 | tf_op jit(solution)/shard_map/psum | solution.py:112
  538.9 30.2 %all-gather.11.cloned.1.call-done = f32[64,8192]{1,0:T(8,128)} async-done(((f32[64,512]{1,0:T(8,128)}), f32[64,8192]{1,0:T(8,128)}) %all-gather.11.cloned.1.call-update) | async-done | bytes 2097168 | tf_op jit(solution)/shard_map/all_gather | solution.py:35
  572.4 57.3 %all-gather.9.cloned.1.call-done = f32[64,8192]{1,0:T(8,128)} async-done(((f32[64,512]{1,0:T(8,128)}), f32[64,8192]{1,0:T(8,128)}) %all-gather.9.cloned.1.call-update) | async-done | bytes 2097168 | tf_op jit(solution)/shard_map/all_gather | solution.py:36
  634.8 17.8 %while.87 = (s32[]{:T(128)}, f32[64,32,256]{2,1,0:T(8,128)S(1)}, f32[64,32,256]{2,1,0:T(8,128)}, s32[]{:T(128)}, s32[40]{0:T(128)S(1)}, /*index=5*/s32[40]{0:T(1...) while((s32[]{:T(128)}, f32[64,32,256]{2,1,0:T(8,128)S(1)}, ...), condition=%wide.region_8.10_spmd, body=%wide.region_7.9_spmd.sunk | while | flops 907545280 | bytes 17834760 | solution.py:74
  659.8 207.3 %while.89 = (s32[]{:T(128)}, f32[64,512]{1,0:T(8,128)S(1)}, s32[]{:T(128)}, f32[64,16,512]{2,1,0:T(8,128)}, s32[]{:T(128)}, /*index=5*/s32[]{:T(128)}, s32[]{:T(128)}, s32[]{:T(128)}) while((s32[]{:T(128)}, f32[64,512]{1,0:T(8,128)S(1)}, s32[]{:T(128)}, f32[64,16,512]{2,1,0:T(8,128)}, s32[]{:T(128)}, /*index=5*/s32[]{:T(128)}, s32[]{:T(128)}, ...), condition=%wide.region_12.14_spmd, body=%wide.region_11.13_spmd.sunk | while | flops 32785 | bytes 1179932 | solution.py:106
  662.7 75.0 %collective-permute-done.3 = f32[64,512]{1,0:T(8,128)S(1)} collective-permute-done((f32[64,512]{1,0:T(8,128)S(1)}, f32[64,512]{1,0:T(8,128)S(1)}, u32[]{:S(2)}, u32[]{:S(2)}) %collective-permute-start.3) | collective-permute-done | bytes 131104 | tf_op jit(solution)/shard_map/while/body/eval_jaxpr/ppermute | solution.py:11
  739.2 7.0 collective-permute-done.3
  747.7 6.7 collective-permute-done.3
  755.9 7.0 collective-permute-done.3
  764.4 8.4 collective-permute-done.3
  774.3 7.3 collective-permute-done.3
  783.1 6.7 collective-permute-done.3
  791.2 7.9 collective-permute-done.3
  800.6 7.4 collective-permute-done.3
  809.6 8.0 collective-permute-done.3
  819.1 8.1 collective-permute-done.3
  828.7 8.0 collective-permute-done.3
  838.2 8.0 collective-permute-done.3
  847.7 8.0 collective-permute-done.3
  857.1 9.9 collective-permute-done.3
  867.1 106.6 %while.88 = (s32[]{:T(128)}, f32[64,512]{1,0:T(8,128)S(1)}, s32[]{:T(128)}, f32[64,16,512]{2,1,0:T(8,128)}, s32[]{:T(128)}, /*index=5*/s32[]{:T(128)}, s32[]{:T(128)}, s32[]{:T(128)}) while((s32[]{:T(128)}, f32[64,512]{1,0:T(8,128)S(1)}, s32[]{:T(128)}, f32[64,16,512]{2,1,0:T(8,128)}, s32[]{:T(128)}, /*index=5*/s32[]{:T(128)}, s32[]{:T(128)}, ...), condition=%wide.region_10.12_spmd, body=%wide.region_9.11_spmd.sunk | while | flops 32785 | bytes 1179932 | solution.py:105
  867.1 8.5 collective-permute-start.2
  886.3 14.2 %collective-permute-start.2 = (f32[64,512]{1,0:T(8,128)S(1)}, f32[64,512]{1,0:T(8,128)S(1)}, u32[]{:S(2)}, u32[]{:S(2)}) collective-permute-start(f32[64,512]{1,0:T(8,128)S(1)} %get-tuple-element.1116), channel_id=1, source_target_pairs={{0,1},{1,2},{2,3},{3,4},{4,5},{5,6},{6,7},{7,8},{8,9},{9,10},{10,1... | collective-permute-start | bytes 393224 | tf_op jit(solution)/shard_map/while/body/eval_jaxpr/ppermute | solution.py:11
  974.3 76.6 %psum.15 = f32[3,64,64]{1,2,0:T(8,128)S(1)} all-reduce(f32[3,64,64]{1,2,0:T(8,128)S(1)} %pad_maximum_fusion.1), channel_id=1, replica_groups=mesh['row'=16,'col'=16] {'row','col'}, use_global_device_ids=true, to_apply=%region_13.15 | all-reduce | flops 12288 | bytes 98304 | tf_op jit(solution)/shard_map/psum | solution.py:121
  (280 shorter events, 277.9 us)
Async XLA Ops:
  7.2 43.1 %all-gather.7.cloned.1.call-start = ((), (), s32[]{:S(2)}) async-start(), calls=%async_computation.1 | async-start | bytes 2228224 | tf_op jit(solution)/shard_map/all_gather | solution.py:35
  7.9 102.4 %all-gather.5.cloned.1.call-start = ((), (), s32[]{:S(2)}) async-start(), calls=%async_computation | async-start | bytes 2228224 | tf_op jit(solution)/shard_map/all_gather | solution.py:36
  8.6 560.5 %all-gather.11.cloned.1.call-start = ((), (), s32[]{:S(2)}) async-start(), calls=%async_computation.3 | async-start | bytes 2228224 | tf_op jit(solution)/shard_map/all_gather | solution.py:35
  140.4 78.7 %collective-permute-start.1 = (f32[64,512]{1,0:T(8,128)S(1)}, f32[64,512]{1,0:T(8,128)S(1)}, u32[]{:S(2)}, u32[]{:S(2)}) collective-permute-start(f32[64,512]{1,0:T(8,128)S(1)} %get-tuple-element.1050), channel_id=1, source_target_pairs={{0,16},{16,32},{32,48},{48,64},{64,80},{80,96},{96,112},{112,128},... | collective-permute-start | bytes 393224 | tf_op jit(solution)/shard_map/while/body/eval_jaxpr/ppermute | solution.py:11
  219.1 8.1 collective-permute-start.1
  227.3 8.1 collective-permute-start.1
  235.4 8.1 collective-permute-start.1
  243.6 9.4 collective-permute-start.1
  253.0 9.3 collective-permute-start.1
  262.3 8.1 collective-permute-start.1
  270.5 8.8 collective-permute-start.1
  279.3 9.1 collective-permute-start.1
  288.4 8.9 collective-permute-start.1
  297.4 8.1 collective-permute-start.1
  305.5 8.2 collective-permute-start.1
  313.8 8.2 collective-permute-start.1
  322.0 10.0 collective-permute-start.1
  332.1 11.9 %collective-permute-start.1 = (f32[64,512]{1,0:T(8,128)S(1)}, f32[64,512]{1,0:T(8,128)S(1)}, u32[]{:S(2)}, u32[]{:S(2)}) collective-permute-start(f32[64,512]{1,0:T(8,128)S(1)} %get-tuple-element.1050), channel_id=1, source_target_pairs={{0,16},{16,32},{32,48},{48,64},{64,80},{80,96},{96,112},{112,128},... | collective-permute-start | bytes 393224 | tf_op jit(solution)/shard_map/while/body/eval_jaxpr/ppermute | solution.py:11
  344.0 25.9 %collective-permute-start = (f32[64,512]{1,0:T(8,128)S(1)}, f32[64,512]{1,0:T(8,128)S(1)}, u32[]{:S(2)}, u32[]{:S(2)}) collective-permute-start(f32[64,512]{1,0:T(8,128)S(1)} %get-tuple-element.1026), channel_id=1, source_target_pairs={{0,1},{1,2},{2,3},{3,4},{4,5},{5,6},{6,7},{7,8},{8,9},{9,10},{10,1... | collective-permute-start | bytes 393224 | tf_op jit(solution)/shard_map/while/body/eval_jaxpr/ppermute | solution.py:11
  386.8 6.6 collective-permute-start
  393.4 6.6 collective-permute-start
  400.0 6.6 collective-permute-start
  406.7 6.6 collective-permute-start
  413.3 6.6 collective-permute-start
  419.9 6.6 collective-permute-start
  426.5 6.6 collective-permute-start
  433.1 6.6 collective-permute-start
  439.7 6.6 collective-permute-start
  446.3 6.6 collective-permute-start
  453.0 6.6 collective-permute-start
  537.1 92.6 %all-gather.9.cloned.1.call-start = ((), (), s32[]{:S(2)}) async-start(), calls=%async_computation.2 | async-start | bytes 2228224 | tf_op jit(solution)/shard_map/all_gather | solution.py:36
  659.8 78.0 %collective-permute-start.3 = (f32[64,512]{1,0:T(8,128)S(1)}, f32[64,512]{1,0:T(8,128)S(1)}, u32[]{:S(2)}, u32[]{:S(2)}) collective-permute-start(f32[64,512]{1,0:T(8,128)S(1)} %get-tuple-element.1140), channel_id=1, source_target_pairs={{0,16},{16,32},{32,48},{48,64},{64,80},{80,96},{96,112},{112,128},... | collective-permute-start | bytes 393224 | tf_op jit(solution)/shard_map/while/body/eval_jaxpr/ppermute | solution.py:11
  737.8 8.4 collective-permute-start.3
  746.2 8.2 collective-permute-start.3
  754.4 8.5 collective-permute-start.3
  763.0 9.8 collective-permute-start.3
  772.8 8.7 collective-permute-start.3
  781.6 8.1 collective-permute-start.3
  789.8 9.4 collective-permute-start.3
  799.2 8.9 collective-permute-start.3
  808.1 9.5 collective-permute-start.3
  817.6 9.6 collective-permute-start.3
  827.2 9.5 collective-permute-start.3
  836.7 9.4 collective-permute-start.3
  846.2 9.4 collective-permute-start.3
  855.7 11.4 %collective-permute-start.3 = (f32[64,512]{1,0:T(8,128)S(1)}, f32[64,512]{1,0:T(8,128)S(1)}, u32[]{:S(2)}, u32[]{:S(2)}) collective-permute-start(f32[64,512]{1,0:T(8,128)S(1)} %get-tuple-element.1140), channel_id=1, source_target_pairs={{0,16},{16,32},{32,48},{48,64},{64,80},{80,96},{96,112},{112,128},... | collective-permute-start | bytes 393224 | tf_op jit(solution)/shard_map/while/body/eval_jaxpr/ppermute | solution.py:11
  867.1 12.5 %collective-permute-start.2 = (f32[64,512]{1,0:T(8,128)S(1)}, f32[64,512]{1,0:T(8,128)S(1)}, u32[]{:S(2)}, u32[]{:S(2)}) collective-permute-start(f32[64,512]{1,0:T(8,128)S(1)} %get-tuple-element.1116), channel_id=1, source_target_pairs={{0,1},{1,2},{2,3},{3,4},{4,5},{5,6},{6,7},{7,8},{8,9},{9,10},{10,1... | collective-permute-start | bytes 393224 | tf_op jit(solution)/shard_map/while/body/eval_jaxpr/ppermute | solution.py:11
  886.3 16.1 %collective-permute-start.2 = (f32[64,512]{1,0:T(8,128)S(1)}, f32[64,512]{1,0:T(8,128)S(1)}, u32[]{:S(2)}, u32[]{:S(2)}) collective-permute-start(f32[64,512]{1,0:T(8,128)S(1)} %get-tuple-element.1116), channel_id=1, source_target_pairs={{0,1},{1,2},{2,3},{3,4},{4,5},{5,6},{6,7},{7,8},{8,9},{9,10},{10,1... | collective-permute-start | bytes 393224 | tf_op jit(solution)/shard_map/while/body/eval_jaxpr/ppermute | solution.py:11
  (22 other events, 511.0 us)
Sparse Core Ops, SparseCore 0:
  9.8 40.3 all-gather.6
  52.7 57.5 all-gather.4
  537.2 31.9 all-gather.10
  572.1 57.5 all-gather.8
where the time goes:
time: 1060 us
  waiting for transfers between devices  639 us (60%)
  blocking collectives  153 us (14%)
  local copies, waits for them, and re-layouts  121 us (11%)
  starting transfers between devices  97.7 us (9%)
  matrix products  28.2 us (3%)
  between operations  14.7 us (1%)
    ppermute x60, waiting for transfers between devices, passed_along(): lax.ppermute(array, axis, [(i, (i + by) % size) for i in range(size)])  452 us
    all_gather x2, waiting for transfers between devices, expand(): far_vec = lax.all_gather(vectors, 'row', axis=1, tiled=True)  114 us
    ppermute x60, starting transfers between devices, passed_along(): lax.ppermute(array, axis, [(i, (i + by) % size) for i in range(size)])  97.5 us
    dynamic_slice x64, local copies, waits for them, and re-layouts, select_piece(): return lax.dynamic_index_in_dim(pieces, position, 1, keepdims=False)  85.7 us
    psum x1, blocking collectives, on_device(): lax.psum(jnp.stack([cross_term, resid_term, square_term]), ('row', 'col'))  76.6 us
    psum x1, blocking collectives, on_device(): rayleigh = lax.psum(first_term, ('row', 'col')) / total_rows  76.2 us
    all_gather x2, waiting for transfers between devices, expand(): near_vec = lax.all_gather(vectors, 'col', axis=1, tiled=True)  71.1 us
  transfers between devices with their start and end apart: 64, of which 64 were waited for; matrix products, arithmetic and copies ran while one was open for 8% of the time, Pallas kernels for 0%

commit v1 on v0

v1 whole, which is shorter than its diff:
```python
import functools

import jax
import jax.numpy as jnp
from jax import lax
from jax.experimental import pallas as pl
from jax.experimental.pallas import tpu as pltpu
from jax.sharding import PartitionSpec as P

MESH = pl.DeviceIdType.MESH
HIGHEST = lax.Precision.HIGHEST
F32 = jnp.float32
BF16 = jnp.bfloat16
RING = 4
VMEM_LIMIT = 60 * 1024 * 1024


class Place:
    def __init__(self):
        row = lax.axis_index("row")
        col = lax.axis_index("col")
        self.x, self.zh = lax.div(row, RING), lax.rem(row, RING)
        self.y = lax.div(col, RING)
        rest = lax.rem(col, RING)
        self.zl, self.core = lax.div(rest, 2), lax.rem(rest, 2)
        self.row, self.col = row, col

    def turn(self, value, by):
        return lax.rem(value + by, RING)

    def row_at(self, dx=0, dz=0):
        return self.turn(self.x, dx) * RING + self.turn(self.zh, dz)

    def col_at(self, dy=0, flip_zl=False, flip_core=False):
        zl = 1 - self.zl if flip_zl else self.zl
        core = 1 - self.core if flip_core else self.core
        return (self.turn(self.y, dy) * 2 + zl) * 2 + core

    def peer(self, dx=0, dz=0, dy=0, flip_zl=False, flip_core=False):
        return (self.row_at(dx, dz), self.col_at(dy, flip_zl, flip_core))


class Wires:
    def __init__(self, place, send_sems, recv_sems):
        self.place, self.send_sems, self.recv_sems = place, send_sems, recv_sems
        self.sent = []

    def send(self, src, dst, peer):
        number = len(self.sent)
        copy = pltpu.make_async_remote_copy(
            src_ref=src,
            dst_ref=dst,
            send_sem=self.send_sems.at[number],
            recv_sem=self.recv_sems.at[number],
            device_id=peer,
            device_id_type=MESH,
        )
        copy.start()
        self.sent.append(copy)
        return number

    def arrived(self, number, landing):
        pltpu.make_async_remote_copy(
            src_ref=landing,
            dst_ref=landing,
            send_sem=self.send_sems.at[number],
            recv_sem=self.recv_sems.at[number],
            device_id=self.place.peer(flip_core=True),
            device_id_type=MESH,
        ).wait_recv()

    def drain(self):
        for copy in self.sent:
            copy.wait_send()


def greet(peers):
    barrier = pltpu.get_barrier_semaphore()
    for peer in peers:
        pl.semaphore_signal(barrier, inc=1, device_id=peer, device_id_type=MESH)
    pl.semaphore_wait(barrier, len(peers))


def near_peers(place):
    return [
        place.peer(dx=1),
        place.peer(dx=3),
        place.peer(dz=1),
        place.peer(dz=3),
        place.peer(dy=1),
        place.peer(dy=3),
        place.peer(flip_zl=True),
        place.peer(flip_core=True),
    ]


def sum_peers(place):
    return [place.peer(dx=2), place.peer(dz=2), place.peer(dy=2)]


def gather(place, wires, own, near, far):
    send, arrived = wires.send, wires.arrived

    def far_at(u, dx=0, dz=0):
        return far.at[place.row_at(dx, dz) * 2 + u]

    def near_at(u, dy=0, flip_zl=False, flip_core=False):
        return near.at[place.col_at(dy, flip_zl, flip_core) * 2 + u]

    xp, xm = place.peer(dx=1), place.peer(dx=3)
    zp, zm = place.peer(dz=1), place.peer(dz=3)
    yp, ym = place.peer(dy=1), place.peer(dy=3)
    zl_peer, core_peer = place.peer(flip_zl=True), place.peer(flip_core=True)

    zp_own, zm_own, zl_own = {}, {}, {}
    to_xp, to_xm, fwd_xp, fwd_xm = {}, {}, {}, {}
    to_yp, to_ym, fwd_yp, fwd_ym = {}, {}, {}, {}
    shared = {}

    def x_out(dz, u, src):
        to_xp[dz, u] = send(src, far_at(u, dz=dz), xp)
        to_xm[dz, u] = send(src, far_at(u, dz=dz), xm)

    def y_out(flip, u, src):
        to_yp[flip, u] = send(src, near_at(u, flip_zl=flip), yp)
        to_ym[flip, u] = send(src, near_at(u, flip_zl=flip), ym)

    def share(dy, flip, u, src):
        shared[dy, flip, u] = send(src, near_at(u, dy, flip), core_peer)

    for u in range(2):
        zl_own[u] = send(own(u), near_at(u), zl_peer)
        zp_own[u] = send(own(u), far_at(u), zp)
        zm_own[u] = send(own(u), far_at(u), zm)
        x_out(0, u, own(u))
        y_out(False, u, own(u))
        share(0, False, u, own(u))
    yield

    def x_in(dz):
        arrived(to_xp[dz, 0], far_at(0, dx=3, dz=dz))
        fwd_xp[dz] = send(far_at(0, dx=3, dz=dz), far_at(0, dx=3, dz=dz), xp)
        arrived(to_xm[dz, 1], far_at(1, dx=1, dz=dz))
        fwd_xm[dz] = send(far_at(1, dx=1, dz=dz), far_at(1, dx=1, dz=dz), xm)

    def y_in(flip):
        arrived(to_yp[flip, 0], near_at(0, 3, flip))
        fwd_yp[flip] = send(near_at(0, 3, flip), near_at(0, 3, flip), yp)
        share(3, flip, 0, near_at(0, 3, flip))
        arrived(to_ym[flip, 1], near_at(1, 1, flip))
        fwd_ym[flip] = send(near_at(1, 1, flip), near_at(1, 1, flip), ym)
        share(1, flip, 1, near_at(1, 1, flip))

    def y_rest(flip):
        arrived(to_ym[flip, 0], near_at(0, 1, flip))
        share(1, flip, 0, near_at(0, 1, flip))
        arrived(to_yp[flip, 1], near_at(1, 3, flip))
        share(3, flip, 1, near_at(1, 3, flip))

    def y_far(flip):
        arrived(fwd_yp[flip], near_at(0, 2, flip))
        share(2, flip, 0, near_at(0, 2, flip))
        arrived(fwd_ym[flip], near_at(1, 2, flip))
        share(2, flip, 1, near_at(1, 2, flip))

    for u in range(2):
        arrived(zl_own[u], near_at(u, flip_zl=True))
        y_out(True, u, near_at(u, flip_zl=True))
        share(0, True, u, near_at(u, flip_zl=True))
    x_in(0)
    y_in(False)
    arrived(zp_own[0], far_at(0, dz=3))
    fwd_zp = send(far_at(0, dz=3), far_at(0, dz=3), zp)
    x_out(3, 0, far_at(0, dz=3))
    arrived(zm_own[0], far_at(0, dz=1))
    x_out(1, 0, far_at(0, dz=1))
    arrived(zm_own[1], far_at(1, dz=1))
    fwd_zm = send(far_at(1, dz=1), far_at(1, dz=1), zm)
    x_out(1, 1, far_at(1, dz=1))
    arrived(zp_own[1], far_at(1, dz=3))
    x_out(3, 1, far_at(1, dz=3))
    y_rest(False)
    y_in(True)
    arrived(fwd_zp, far_at(0, dz=2))
    x_out(2, 0, far_at(0, dz=2))
    arrived(fwd_zm, far_at(1, dz=2))
    x_out(2, 1, far_at(1, dz=2))
    x_in(3)
    x_in(1)
    y_far(False)
    y_rest(True)
    y_far(True)
    x_in(2)
    for dz in (0, 3, 1, 2):
        arrived(to_xm[dz, 0], far_at(0, dx=1, dz=dz))
        arrived(to_xp[dz, 1], far_at(1, dx=3, dz=dz))
        arrived(fwd_xp[dz], far_at(0, dx=2, dz=dz))
        arrived(fwd_xm[dz], far_at(1, dx=2, dz=dz))
    for (dy, flip, u), number in shared.items():
        arrived(number, near_at(u, dy, flip, True))
    yield


class RingSum:
    def __init__(self, wires, term, box, pair, plus, minus):
        self.wires, self.term, self.box, self.pair = wires, term, box, pair
        self.plus, self.minus = plus, minus

    def opposite(self):
        send = self.wires.send
        self.opp = (
            send(self.term(2, 0), self.box(0), self.plus),
            send(self.term(2, 1), self.box(1), self.minus),
        )

    def plain(self):
        send = self.wires.send
        self.flat = (
            send(self.term(1, 1), self.box(2), self.plus),
            send(self.term(3, 0), self.box(3), self.minus),
        )

    def joined(self):
        send, arrived = self.wires.send, self.wires.arrived
        arrived(self.opp[0], self.box(0))
        self.pair(0)[...] = self.term(1, 0)[...] + self.box(0)[...]
        first = send(self.pair(0), self.box(4), self.plus)
        arrived(self.opp[1], self.box(1))
        self.pair(1)[...] = self.term(3, 1)[...] + self.box(1)[...]
        second = send(self.pair(1), self.box(5), self.minus)
        self.both = (first, second)

    def total(self):
        arrived = self.wires.arrived
        arrived(self.flat[0], self.box(2))
        arrived(self.flat[1], self.box(3))
        arrived(self.both[0], self.box(4))
        arrived(self.both[1], self.box(5))
        low = self.term(0, 0)[...] + (self.box(4)[...] + self.box(3)[...])
        high = self.term(0, 1)[...] + (self.box(2)[...] + self.box(5)[...])
        return low, high


class SmallSum:
    def __init__(self, place, wires, slots):
        self.place, self.wires, self.slots = place, wires, slots

    def pair_out(self, stage, value, mine, peer):
        self.mine = mine
        self.slots[stage, mine] = value
        self.numbers = [self.wires.send(self.slots.at[stage, mine], self.slots.at[stage, mine], peer)]

    def pair_in(self, stage):
        self.wires.arrived(self.numbers[0], self.slots.at[stage, 1 - self.mine])
        return self.slots[stage, 0] + self.slots[stage, 1]

    def ring_out(self, stage, value, mine, peers):
        self.mine = mine
        self.slots[stage, mine] = value
        self.numbers = [
            self.wires.send(self.slots.at[stage, mine], self.slots.at[stage, mine], peers[by])
            for by in (1, 2, 3)
        ]

    def ring_in(self, stage):
        for number, by in zip(self.numbers, (1, 2, 3)):
            origin = lax.rem(self.mine + RING - by, RING)
            self.wires.arrived(number, self.slots.at[stage, origin])
        return (self.slots[stage, 0] + self.slots[stage, 1]) + (self.slots[stage, 2] + self.slots[stage, 3])

    def run(self, value):
        place = self.place
        self.pair_out(0, value, place.core, place.peer(flip_core=True))
        yield None
        value = self.pair_in(0)
        self.pair_out(1, value, place.zl, place.peer(flip_zl=True))
        yield None
        value = self.pair_in(1)
        self.ring_out(2, value, place.y, {by: place.peer(dy=by) for by in (1, 2, 3)})
        yield None
        value = self.ring_in(2)
        self.ring_out(3, value, place.x, {by: place.peer(dx=by) for by in (1, 2, 3)})
        yield None
        value = self.ring_in(3)
        self.ring_out(4, value, place.zh, {by: place.peer(dz=by) for by in (1, 2, 3)})
        yield None
        yield self.ring_in(4)


def reduce_all(place, wires, small, part_rows, part_cols, boxes, make_small):
    core_box, near_sum, y_box, y_pair, y_held, zl_box, x_box, x_pair, x_held, z_box, z_pair = boxes
    send, arrived = wires.send, wires.arrived
    xp, xm = place.peer(dx=1), place.peer(dx=3)
    zp, zm = place.peer(dz=1), place.peer(dz=3)
    yp, ym = place.peer(dy=1), place.peer(dy=3)
    zl_peer, core_peer = place.peer(flip_zl=True), place.peer(flip_core=True)

    def x_ring(k, dz):
        return RingSum(
            wires,
            lambda d, u: part_cols.at[place.row_at(d, dz) * 2 + u],
            lambda i: x_box.at[k, i],
            lambda i: x_pair.at[k, i],
            xp,
            xm,
        )

    depths = (2, 1, 3, 0)
    x_rings = [x_ring(k, dz) for k, dz in enumerate(depths)]
    crossed = {}
    x_rings[0].opposite()
    x_rings[1].opposite()
    for dy in (2, 1, 3, 0):
        for flip in (True, False):
            source = place.col_at(dy, flip, True) * 2
            crossed[dy, flip] = send(
                part_rows.at[pl.ds(source, 2)], core_box.at[dy, int(flip)], core_peer
            )
    x_rings[0].plain()
    sums = small.run(make_small())
    next(sums)

    def y_ring(flip):
        return RingSum(
            wires,
            lambda d, u: near_sum.at[d, int(flip), u],
            lambda i: y_box.at[int(flip), i],
            lambda i: y_pair.at[int(flip), i],
            yp,
            ym,
        )

    y_rings = {flip: y_ring(flip) for flip in (True, False)}

    def cross(dy, flip):
        arrived(crossed[dy, flip], core_box.at[dy, int(flip)])
        source = place.col_at(dy, flip) * 2
        near_sum[dy, int(flip)] = part_rows[pl.ds(source, 2)] + core_box[dy, int(flip)]

    for flip in (True, False):
        cross(2, flip)
        y_rings[flip].opposite()
    x_rings[0].joined()
    x_rings[2].opposite()
    x_rings[1].plain()
    for flip in (True, False):
        cross(1, flip)
        cross(3, flip)
        y_rings[flip].plain()
    next(sums)
    x_rings[1].joined()
    x_rings[3].opposite()
    x_rings[2].plain()
    y_rings[True].joined()
    for flip in (True, False):
        cross(0, flip)
    next(sums)
    y_rings[False].joined()

    def hold_x(k):
        x_held[k, 0], x_held[k, 1] = x_rings[k].total()

    z_ring = RingSum(
        wires,
        lambda d, u: x_held.at[depths.index(d), u],
        lambda i: z_box.at[i],
        lambda i: z_pair.at[i],
        zp,
        zm,
    )
    hold_x(0)
    z_ring.opposite()
    x_rings[2].joined()
    x_rings[3].plain()
    next(sums)
    y_held[1, 0], y_held[1, 1] = y_rings[True].total()
    zl_sent = send(y_held.at[1], zl_box, zl_peer)
    x_rings[3].joined()
    y_held[0, 0], y_held[0, 1] = y_rings[False].total()
    hold_x(1)
    hold_x(2)
    z_ring.plain()
    next(sums)
    z_ring.joined()
    arrived(zl_sent, zl_box)
    small_total = next(sums)
    hold_x(3)
    low, high = z_ring.total()
    halves = (
        low + (y_held[0, 0] + zl_box[0]),
        high + (y_held[0, 1] + zl_box[1]),
    )
    return halves, small_total


def reduce_scratch(K, T, rows):
    return [
        pltpu.VMEM((4, 2, 2, K, T), F32),
        pltpu.VMEM((4, 2, 2, K, T), F32),
        pltpu.VMEM((2, 6, K, T), F32),
        pltpu.VMEM((2, 2, K, T), F32),
        pltpu.VMEM((2, 2, K, T), F32),
        pltpu.VMEM((2, K, T), F32),
        pltpu.VMEM((4, 6, K, T), F32),
        pltpu.VMEM((4, 2, K, T), F32),
        pltpu.VMEM((4, 2, K, T), F32),
        pltpu.VMEM((6, K, T), F32),
        pltpu.VMEM((2, K, T), F32),
        pltpu.VMEM((5, 4, rows, 2 * K), F32),
    ]


def split(value):
    high = value.astype(BF16)
    low = (value - high.astype(F32)).astype(BF16)
    return high, low


def dot_t(left, right, precision=None):
    return lax.dot_general(
        left, right, (((1,), (1,)), ((), ())), precision=precision, preferred_element_type=F32
    )


def dot_n(left, right, precision=None):
    return lax.dot_general(
        left, right, (((1,), (0,)), ((), ())), precision=precision, preferred_element_type=F32
    )


def fold(square):
    half = square.shape[0] // 2
    return jnp.concatenate([square[:half], square[half:]], axis=1)


def unfold(flat):
    half = flat.shape[1] // 2
    return jnp.concatenate([flat[:, :half], flat[:, half:]], axis=0)


def energy(part_rows, near):
    K = part_rows.shape[1]

    def step(p, total):
        left = jnp.concatenate(split(part_rows[p]), axis=0)
        right = jnp.concatenate(split(near[p]), axis=0)
        return total + dot_t(left, right)

    total = lax.fori_loop(0, part_rows.shape[0], step, jnp.zeros((2 * K, 2 * K), F32))
    total = total[:K] + total[K:]
    total = total[:, :K] + total[:, K:]
    return total + total.T


def first_kernel(block, near, far, send_sems, recv_sems):
    place = Place()
    K, width = block.shape
    T = width // 2
    greet(near_peers(place))
    wires = Wires(place, send_sems, recv_sems)
    steps = gather(place, wires, lambda u: block.at[:, pl.ds(u * T, T)], near, far)
    next(steps)
    for u in range(2):
        half = block[:, u * T : (u + 1) * T]
        near[place.col * 2 + u] = half
        far[place.row * 2 + u] = half
    next(steps)
    wires.drain()


def middle_kernel(
    total_rows, block, near_x, part_rows, part_cols, image, rayleigh, grams, near, far, *scratch
):
    *boxes, slots, resid, send_sems, recv_sems = scratch
    place = Place()
    K, width = block.shape
    T = width // 2
    greet(near_peers(place) + sum_peers(place))
    wires = Wires(place, send_sems, recv_sems)
    small = SmallSum(place, wires, slots)
    halves, total = reduce_all(
        place, wires, small, part_rows, part_cols, boxes, lambda: fold(energy(part_rows, near_x))
    )
    mean = unfold(total) / total_rows
    for u in range(2):
        resid[u] = halves[u] - dot_n(mean, block[:, u * T : (u + 1) * T], HIGHEST)
    steps = gather(place, wires, lambda u: resid.at[u], near, far)
    next(steps)
    rayleigh[...] = mean
    cross = jnp.zeros((K, K), F32)
    square = jnp.zeros((K, K), F32)
    for u in range(2):
        image[:, u * T : (u + 1) * T] = halves[u]
        value = resid[u]
        near[place.col * 2 + u] = value
        far[place.row * 2 + u] = value
        cross += dot_t(halves[u], value, HIGHEST)
        square += dot_t(value, value, HIGHEST)
    grams[0] = cross
    grams[1] = square
    next(steps)
    wires.drain()


def last_kernel(
    total_rows, rayleigh, local_grams, near_w, part_rows, part_cols, image, grams, *scratch
):
    *boxes, slots, send_sems, recv_sems = scratch
    place = Place()
    T = part_rows.shape[2]
    half = rayleigh.shape[0] // 2
    greet(near_peers(place) + sum_peers(place))
    wires = Wires(place, send_sems, recv_sems)
    small = SmallSum(place, wires, slots)

    def make_small():
        return jnp.concatenate(
            [
                fold(local_grams[0]),
                fold(energy(part_rows, near_w)),
                fold(local_grams[1]),
            ],
            axis=0,
        )

    halves, total = reduce_all(place, wires, small, part_rows, part_cols, boxes, make_small)
    for u in range(2):
        image[:, u * T : (u + 1) * T] = halves[u]
    grams[0] = rayleigh[...]
    for i in range(3):
        grams[1 + i] = unfold(total[i * half : (i + 1) * half]) / total_rows
    wires.drain()


def tile_kernel(
    count, row_ids, col_ids, tiles, near, far, part_rows, part_cols, held, near_two, far_two, sems
):
    slots = tiles.shape[0]
    live = count[0]

    def fetch(s):
        return pltpu.make_async_copy(tiles.at[s], held.at[s], sems.at[s])

    for s in range(slots):
        fetch(s).start()
    zero = jnp.zeros(part_rows.shape[1:], F32)

    def prepare(p, carry):
        part_rows[p] = zero
        part_cols[p] = zero
        near_two[p] = jnp.concatenate(split(near[p]), axis=0)
        far_two[p] = jnp.concatenate(split(far[p]), axis=0)
        return carry

    lax.fori_loop(0, part_rows.shape[0], prepare, 0)
    K = near.shape[1]

    def step(s, carry):
        fetch(s).wait()
        row, col = row_ids[s], col_ids[s]
        high, low = split(held[s])
        rows_in, cols_in = near_two[row], far_two[col]
        lower = dot_t(cols_in, high)
        upper = dot_n(rows_in, high)
        part_rows[row] += (lower[:K] + lower[K:]) + dot_t(cols_in[:K], low)
        part_cols[col] += (upper[:K] + upper[K:]) + dot_n(rows_in[:K], low)
        return carry

    lax.fori_loop(0, live, step, 0)

    def finish(s, carry):
        fetch(s).wait()
        return carry

    lax.fori_loop(live, slots, finish, 0)


def vmem(count):
    return [pl.BlockSpec(memory_space=pltpu.VMEM)] * count


def on_device(tile_count, tile_rows, tile_cols, tiles, block):
    K, width = block.shape
    T = tiles.shape[-1]
    slots = tiles.shape[2]
    total_rows = width * lax.axis_size("row") * lax.axis_size("col")
    count, row_ids, col_ids = tile_count[0], tile_rows[0, 0], tile_cols[0, 0]
    data = tiles[0, 0]
    strip = jax.ShapeDtypeStruct((32, K, T), F32)
    seg = jax.ShapeDtypeStruct((K, width), F32)

    def params(number):
        return pltpu.CompilerParams(
            collective_id=number, has_side_effects=True, vmem_limit_bytes=VMEM_LIMIT
        )

    def sems(count):
        return [pltpu.SemaphoreType.DMA((count,)), pltpu.SemaphoreType.DMA((count,))]

    near, far = pl.pallas_call(
        first_kernel,
        out_shape=(strip, strip),
        in_specs=vmem(1),
        out_specs=tuple(vmem(2)),
        scratch_shapes=sems(60),
        compiler_params=params(0),
        name="gather_block",
    )(block)

    def products(near, far):
        smem = pl.BlockSpec(memory_space=pltpu.SMEM)
        return pl.pallas_call(
            tile_kernel,
            out_shape=(strip, strip),
            in_specs=[smem, smem, smem, pl.BlockSpec(memory_space=pl.ANY)] + vmem(2),
            out_specs=tuple(vmem(2)),
            scratch_shapes=[
                pltpu.VMEM((slots, T, T), F32),
                pltpu.VMEM((32, 2 * K, T), BF16),
                pltpu.VMEM((32, 2 * K, T), BF16),
                pltpu.SemaphoreType.DMA((slots,)),
            ],
            compiler_params=pltpu.CompilerParams(vmem_limit_bytes=VMEM_LIMIT),
            name="tile_products",
        )(count, row_ids, col_ids, data, near, far)

    part_rows, part_cols = products(near, far)
    image_x, rayleigh, local_grams, near_w, far_w = pl.pallas_call(
        functools.partial(middle_kernel, total_rows),
        out_shape=(
            seg,
            jax.ShapeDtypeStruct((K, K), F32),
            jax.ShapeDtypeStruct((2, K, K), F32),
            strip,
            strip,
        ),
        in_specs=vmem(4),
        out_specs=tuple(vmem(5)),
        scratch_shapes=reduce_scratch(K, T, K // 2) + [pltpu.VMEM((2, K, T), F32)] + sems(136),
        compiler_params=params(1),
        name="reduce_and_gather",
    )(block, near, part_rows, part_cols)
    part_rows, part_cols = products(near_w, far_w)
    image_w, grams = pl.pallas_call(
        functools.partial(last_kernel, total_rows),
        out_shape=(seg, jax.ShapeDtypeStruct((4, K, K), F32)),
        in_specs=vmem(5),
        out_specs=tuple(vmem(2)),
        scratch_shapes=reduce_scratch(K, T, 3 * K // 2) + sems(76),
        compiler_params=params(2),
        name="reduce_last",
    )(rayleigh, local_grams, near_w, part_rows, part_cols)
    return image_x, image_w, grams


def solution(mesh):
    return jax.shard_map(
        on_device,
        mesh=mesh,
        in_specs=(
            P("row", "col"),
            P("row", "col", None),
            P("row", "col", None),
            P("row", "col", None, None, None),
            P(None, ("row", "col")),
        ),
        out_specs=(P(None, ("row", "col")), P(None, ("row", "col")), P()),
        check_vma=False,
    )
```

time: 1060 us -> 172 us (0.16)
  waiting for transfers between devices: 639 us -> 0 us
  Pallas kernels: 0 us -> 168 us
  blocking collectives: 153 us -> 0 us
  local copies, waits for them, and re-layouts: 121 us -> 3.8 us
  starting transfers between devices: 97.7 us -> 0 us
  matrix products: 28.2 us -> 0 us
  between operations: 14.7 us -> 1.33 us
    ppermute x60 -> x0, waiting for transfers between devices: 452 us -> none  [passed_along(): lax.ppermute(array, axis, [(i, (i + by) % size) for i in range(size)])]
    all_gather x4 -> x0, waiting for transfers between devices: 185 us -> none  [the longest x2 114 us: expand(): far_vec = lax.all_gather(vectors, 'row', axis=1, tiled=True)]
    pallas_call x0 -> x5, Pallas kernels: none -> 168 us  [the longest x1 65.4 us: on_device(): pl.pallas_call(functools.partial(middle_kernel, total_rows), out_shape=(s...]
    psum x2 -> x0, blocking collectives: 153 us -> none  [the longest x1 76.6 us: on_device(): lax.psum(jnp.stack([cross_term, resid_term, square_term]), ('row', 'col'))]
    ppermute x60 -> x0, starting transfers between devices: 97.5 us -> none  [passed_along(): lax.ppermute(array, axis, [(i, (i + by) % size) for i in range(size)])]
    dynamic_slice x64 -> x0, local copies, waits for them, and re-layouts: 85.7 us -> none  [select_piece(): return lax.dynamic_index_in_dim(pieces, position, 1, keepdims=False)]
    dot_general x13 -> x0, matrix products: 28.2 us -> none  [the longest x2 8.14 us: accumulate(): jnp.einsum('ksi,sp->kpi', upper_part, col_pick, precision=highest)]
    reshape x4 -> x0, local copies, waits for them, and re-layouts: 12.8 us -> none  [the longest x2 6.42 us: expand(): near_tiles = near_vec.reshape(vec_count, row_slots, tile_size)]
  transfers between devices with their start and end apart: 64 -> 0, of which waited for: 64 -> 0; matrix products, arithmetic and copies ran while one was open for 8% -> 0% of each run, Pallas kernels for 0% -> 0%
where the time goes in v1:
time: 172 us; the launch traced here: 173 us
  Pallas kernels  168 us (98%)
  local copies, waits for them, and re-layouts  3.8 us (2%)
    pallas_call x1, Pallas kernels, on_device(): pl.pallas_call(functools.partial(middle_kernel, total_rows), out_shape=(s...  65.4 us
    pallas_call x1, Pallas kernels, on_device(): pl.pallas_call(functools.partial(last_kernel, total_rows), out_shape=(seg...  49.4 us
    pallas_call x1, Pallas kernels, on_device(): pl.pallas_call(first_kernel, out_shape=(strip, strip), in_specs=vmem(1),...  35.6 us
    pallas_call x2, Pallas kernels, products(): pl.pallas_call(tile_kernel, out_shape=(strip, strip), in_specs=[smem, sme...  17.1 us
    unnamed x5, local copies, waits for them, and re-layouts  3.8 us

profile of v1, /device:TPU:1, one launch (start us, length us, event | category | flops | bytes accessed | tf_op | source)
XLA Modules:
  0.0 172.6 jit_solution(12151247622777877274)
XLA Ops:
  1.3 35.6 %gather_block.1 = (f32[32,64,256]{2,1,0:T(8,128)}, f32[32,64,256]{2,1,0:T(8,128)}) custom-call(f32[64,512]{1,0:T(8,128)} %block.3), custom_call_target="tpu_custom_call" | custom-call | tf_op jit(solution)/shard_map/gather_block/pallas_call | solution.py:600
  36.9 8.6 %tile_products.2 = (f32[32,64,256]{2,1,0:T(8,128)}, f32[32,64,256]{2,1,0:T(8,128)}) custom-call(s32[1]{0:T(128)} %bitcast.4.count, s32[40]{0:T(128)} %bitcast.8, s32[40]{0:T(128)} %bitcast.10, f32[40,256,256]{2,1,0:T(8,128)} %bitcast.6, f32[32,64,256]{2,1,0:T(8,128)} %get-tuple-element.16.near.near_x, f32[32,64,256]{2,1,0:T(8,128)} %get-tuple-element.17.far), custom_call_target="tpu_custom_call" | custom-call | tf_op jit(solution)/shard_map/tile_products/pallas_call | solution.py:612
  45.5 65.4 %reduce_and_gather.1 = (f32[64,512]{1,0:T(8,128)}, f32[64,64]{1,0:T(8,128)}, f32[2,64,64]{2,1,0:T(8,128)}, f32[32,64,256]{2,1,0:T(8,128)}, f32[32,64,256]{2,1,0:T(8,128)}) custom-call(f32[64,512]{1,0:T(8,128)} %block.3, f32[32,64,256]{2,1,0:T(8,128)} %get-tuple-element.16.near.near_x, f32[32,64,256]{2,1,0:T(8,128)} %get-tuple-element.18.part_rows, ...), custom_call_target="tpu_custom_call" | custom-call | tf_op jit(solution)/shard_map/reduce_and_gather/pallas_call | solution.py:628
  110.9 8.5 %tile_products.3 = (f32[32,64,256]{2,1,0:T(8,128)}, f32[32,64,256]{2,1,0:T(8,128)}) custom-call(s32[1]{0:T(128)} %bitcast.5.count, s32[40]{0:T(128)} %bitcast.9, s32[40]{0:T(128)} %bitcast.11, f32[40,256,256]{2,1,0:T(8,128)} %bitcast.7, f32[32,64,256]{2,1,0:T(8,128)} %get-tuple-element.23.near.near_w, f32[32,64,256]{2,1,0:T(8,128)} %get-tuple-element.24.far), custom_call_target="tpu_custom_call" | custom-call | tf_op jit(solution)/shard_map/tile_products/pallas_call | solution.py:612
  119.5 0.0 copy-start
  119.5 49.4 %reduce_last.1 = (f32[64,512]{1,0:T(8,128)}, f32[4,64,64]{2,1,0:T(8,128)}) custom-call(f32[64,64]{1,0:T(8,128)} %get-tuple-element.21.rayleigh, f32[2,64,64]{2,1,0:T(8,128)} %get-tuple-element.22.local_grams, f32[32,64,256]{2,1,0:T(8,128)} %get-tuple-element.23.near.near_w, f32[32,64,256]{2,1,0:T(8,128)} %get-tuple-element.25.part_rows, ...), custom_call_target="tpu_custom_call" | custom-call | tf_op jit(solution)/shard_map/reduce_last/pallas_call | solution.py:644
  168.8 0.0 copy-done
  168.9 0.7 copy.12
  169.5 1.6 copy.13
  171.1 1.6 copy.14
Async XLA Ops:
  119.5 49.4 %copy-start = (f32[64,512]{1,0:T(8,128)S(1)}, f32[64,512]{1,0:T(8,128)}, u32[]{:S(2)}) copy-start(f32[64,512]{1,0:T(8,128)} %get-tuple-element.32) | copy-start | bytes 393220

commit v2 on v1

--- a/solution.py
+++ b/solution.py
@@ -130,10 +130,12 @@
 
     for u in range(2):
         zl_own[u] = send(own(u), near_at(u), zl_peer)
+    for u in range(2):
         zp_own[u] = send(own(u), far_at(u), zp)
         zm_own[u] = send(own(u), far_at(u), zm)
         x_out(0, u, own(u))
         y_out(False, u, own(u))
+    for u in range(2):
         share(0, False, u, own(u))
     yield
 
@@ -167,38 +169,44 @@
         arrived(zl_own[u], near_at(u, flip_zl=True))
         y_out(True, u, near_at(u, flip_zl=True))
         share(0, True, u, near_at(u, flip_zl=True))
+    yield
     x_in(0)
     y_in(False)
     arrived(zp_own[0], far_at(0, dz=3))
     fwd_zp = send(far_at(0, dz=3), far_at(0, dz=3), zp)
     x_out(3, 0, far_at(0, dz=3))
-    arrived(zm_own[0], far_at(0, dz=1))
-    x_out(1, 0, far_at(0, dz=1))
     arrived(zm_own[1], far_at(1, dz=1))
     fwd_zm = send(far_at(1, dz=1), far_at(1, dz=1), zm)
     x_out(1, 1, far_at(1, dz=1))
+    yield
+    arrived(zm_own[0], far_at(0, dz=1))
+    x_out(1, 0, far_at(0, dz=1))
     arrived(zp_own[1], far_at(1, dz=3))
     x_out(3, 1, far_at(1, dz=3))
     y_rest(False)
     y_in(True)
+    yield
+    y_far(False)
+    y_rest(True)
     arrived(fwd_zp, far_at(0, dz=2))
     x_out(2, 0, far_at(0, dz=2))
     arrived(fwd_zm, far_at(1, dz=2))
     x_out(2, 1, far_at(1, dz=2))
     x_in(3)
+    yield
     x_in(1)
-    y_far(False)
-    y_rest(True)
     y_far(True)
+    for (dy, flip, u), number in shared.items():
+        arrived(number, near_at(u, dy, flip, True))
+    yield "near"
     x_in(2)
+    yield
     for dz in (0, 3, 1, 2):
         arrived(to_xm[dz, 0], far_at(0, dx=1, dz=dz))
         arrived(to_xp[dz, 1], far_at(1, dx=3, dz=dz))
         arrived(fwd_xp[dz], far_at(0, dx=2, dz=dz))
         arrived(fwd_xm[dz], far_at(1, dx=2, dz=dz))
-    for (dy, flip, u), number in shared.items():
-        arrived(number, near_at(u, dy, flip, True))
-    yield
+    yield "far"
 
 
 class RingSum:
@@ -287,113 +295,95 @@
         yield self.ring_in(4)
 
 
-def reduce_all(place, wires, small, part_rows, part_cols, boxes, make_small):
-    core_box, near_sum, y_box, y_pair, y_held, zl_box, x_box, x_pair, x_held, z_box, z_pair = boxes
-    send, arrived = wires.send, wires.arrived
-    xp, xm = place.peer(dx=1), place.peer(dx=3)
-    zp, zm = place.peer(dz=1), place.peer(dz=3)
-    yp, ym = place.peer(dy=1), place.peer(dy=3)
-    zl_peer, core_peer = place.peer(flip_zl=True), place.peer(flip_core=True)
-
-    def x_ring(k, dz):
-        return RingSum(
+class Reduction:
+    depths = (2, 1, 3, 0)
+
+    def __init__(self, place, wires, part_rows, part_cols, boxes):
+        self.place, self.wires = place, wires
+        self.part_rows = part_rows
+        (
+            self.core_box,
+            self.near_sum,
+            y_box,
+            y_pair,
+            self.y_held,
+            self.zl_box,
+            x_box,
+            x_pair,
+            self.x_held,
+            z_box,
+            z_pair,
+        ) = boxes
+        xp, xm = place.peer(dx=1), place.peer(dx=3)
+        zp, zm = place.peer(dz=1), place.peer(dz=3)
+        yp, ym = place.peer(dy=1), place.peer(dy=3)
+        self.zl_peer = place.peer(flip_zl=True)
+        self.core_peer = place.peer(flip_core=True)
+
+        def x_ring(k, dz):
+            return RingSum(
+                wires,
+                lambda d, u: part_cols.at[place.row_at(d, dz) * 2 + u],
+                lambda i: x_box.at[k, i],
+                lambda i: x_pair.at[k, i],
+                xp,
+                xm,
+            )
+
+        def y_ring(flip):
+            return RingSum(
+                wires,
+                lambda d, u: self.near_sum.at[d, int(flip), u],
+                lambda i: y_box.at[int(flip), i],
+                lambda i: y_pair.at[int(flip), i],
+                yp,
+                ym,
+            )
+
+        self.x = [x_ring(k, dz) for k, dz in enumerate(self.depths)]
+        self.y = {flip: y_ring(flip) for flip in (True, False)}
+        self.z = RingSum(
             wires,
-            lambda d, u: part_cols.at[place.row_at(d, dz) * 2 + u],
-            lambda i: x_box.at[k, i],
-            lambda i: x_pair.at[k, i],
-            xp,
-            xm,
+            lambda d, u: self.x_held.at[self.depths.index(d), u],
+            lambda i: z_box.at[i],
+            lambda i: z_pair.at[i],
+            zp,
+            zm,
         )
 
-    depths = (2, 1, 3, 0)
-    x_rings = [x_ring(k, dz) for k, dz in enumerate(depths)]
-    crossed = {}
-    x_rings[0].opposite()
-    x_rings[1].opposite()
-    for dy in (2, 1, 3, 0):
-        for flip in (True, False):
-            source = place.col_at(dy, flip, True) * 2
-            crossed[dy, flip] = send(
-                part_rows.at[pl.ds(source, 2)], core_box.at[dy, int(flip)], core_peer
-            )
-    x_rings[0].plain()
-    sums = small.run(make_small())
-    next(sums)
-
-    def y_ring(flip):
-        return RingSum(
-            wires,
-            lambda d, u: near_sum.at[d, int(flip), u],
-            lambda i: y_box.at[int(flip), i],
-            lambda i: y_pair.at[int(flip), i],
-            yp,
-            ym,
-        )
-
-    y_rings = {flip: y_ring(flip) for flip in (True, False)}
-
-    def cross(dy, flip):
-        arrived(crossed[dy, flip], core_box.at[dy, int(flip)])
-        source = place.col_at(dy, flip) * 2
-        near_sum[dy, int(flip)] = part_rows[pl.ds(source, 2)] + core_box[dy, int(flip)]
-
-    for flip in (True, False):
-        cross(2, flip)
-        y_rings[flip].opposite()
-    x_rings[0].joined()
-    x_rings[2].opposite()
-    x_rings[1].plain()
-    for flip in (True, False):
-        cross(1, flip)
-        cross(3, flip)
-        y_rings[flip].plain()
-    next(sums)
-    x_rings[1].joined()
-    x_rings[3].opposite()
-    x_rings[2].plain()
-    y_rings[True].joined()
-    for flip in (True, False):
-        cross(0, flip)
-    next(sums)
-    y_rings[False].joined()
-
-    def hold_x(k):
-        x_held[k, 0], x_held[k, 1] = x_rings[k].total()
-
-    z_ring = RingSum(
-        wires,
-        lambda d, u: x_held.at[depths.index(d), u],
-        lambda i: z_box.at[i],
-        lambda i: z_pair.at[i],
-        zp,
-        zm,
-    )
-    hold_x(0)
-    z_ring.opposite()
-    x_rings[2].joined()
-    x_rings[3].plain()
-    next(sums)
-    y_held[1, 0], y_held[1, 1] = y_rings[True].total()
-    zl_sent = send(y_held.at[1], zl_box, zl_peer)
-    x_rings[3].joined()
-    y_held[0, 0], y_held[0, 1] = y_rings[False].total()
-    hold_x(1)
-    hold_x(2)
-    z_ring.plain()
-    next(sums)
-    z_ring.joined()
-    arrived(zl_sent, zl_box)
-    small_total = next(sums)
-    hold_x(3)
-    low, high = z_ring.total()
-    halves = (
-        low + (y_held[0, 0] + zl_box[0]),
-        high + (y_held[0, 1] + zl_box[1]),
-    )
-    return halves, small_total
-
-
-def reduce_scratch(K, T, rows):
+    def cross_out(self):
+        self.crossed = {}
+        for dy in (2, 1, 3, 0):
+            for flip in (True, False):
+                source = self.place.col_at(dy, flip, True) * 2
+                self.crossed[dy, flip] = self.wires.send(
+                    self.part_rows.at[pl.ds(source, 2)],
+                    self.core_box.at[dy, int(flip)],
+                    self.core_peer,
+                )
+
+    def cross_in(self, dy, flip):
+        self.wires.arrived(self.crossed[dy, flip], self.core_box.at[dy, int(flip)])
+        source = self.place.col_at(dy, flip) * 2
+        self.near_sum[dy, int(flip)] = self.part_rows[pl.ds(source, 2)] + self.core_box[dy, int(flip)]
+
+    def hold_x(self, k):
+        self.x_held[k, 0], self.x_held[k, 1] = self.x[k].total()
+
+    def hold_y(self, flip):
+        self.y_held[int(flip), 0], self.y_held[int(flip), 1] = self.y[flip].total()
+
+    def zl_out(self):
+        self.zl_sent = self.wires.send(self.y_held.at[1], self.zl_box, self.zl_peer)
+
+    def finish(self):
+        self.wires.arrived(self.zl_sent, self.zl_box)
+        near = [self.y_held[0, u] + self.zl_box[u] for u in range(2)]
+        low, high = self.z.total()
+        return low + near[0], high + near[1]
+
+
+def reduce_scratch(K, T):
     return [
         pltpu.VMEM((4, 2, 2, K, T), F32),
         pltpu.VMEM((4, 2, 2, K, T), F32),
@@ -406,7 +396,6 @@
         pltpu.VMEM((4, 2, K, T), F32),
         pltpu.VMEM((6, K, T), F32),
         pltpu.VMEM((2, K, T), F32),
-        pltpu.VMEM((5, 4, rows, 2 * K), F32),
     ]
 
 
@@ -452,127 +441,219 @@
     return total + total.T
 
 
-def first_kernel(block, near, far, send_sems, recv_sems):
+class Application:
+    def __init__(self, place, wires, table, pairs, sums, near, far, part_rows, part_cols, boxes, slots):
+        self.place, self.wires, self.table, self.pairs, self.sums = place, wires, table, pairs, sums
+        self.near, self.far = near, far
+        self.part_rows, self.part_cols = part_rows, part_cols
+        self.slots = slots
+        self.reduction = Reduction(place, wires, part_rows, part_cols, boxes)
+
+    def upper(self, start, stop):
+        K = self.near.shape[1]
+
+        def step(s, carry):
+            high, low = split(self.near[self.table[0, s]])
+            both = dot_n(jnp.concatenate([high, low], axis=0), self.pairs[s, 0])
+            value = (both[:K] + both[K:]) + dot_n(high, self.pairs[s, 1])
+            self.sums[s + 1] = value + self.sums[self.table[3, s]]
+            return carry
+
+        lax.fori_loop(start, stop, step, 0)
+
+    def lower(self, start, stop):
+        K = self.near.shape[1]
+
+        def step(s, carry):
+            high, low = split(self.far[self.table[1, s]])
+            both = dot_t(jnp.concatenate([high, low], axis=0), self.pairs[s, 0])
+            value = (both[:K] + both[K:]) + dot_t(high, self.pairs[s, 1])
+            self.sums[s + 1] = value + self.sums[self.table[2, s]]
+            return carry
+
+        lax.fori_loop(start, stop, step, 0)
+
+    def collect(self, line, parts):
+        def step(p, carry):
+            parts[p] = self.sums[self.table[line, p]]
+            return carry
+
+        lax.fori_loop(0, parts.shape[0], step, 0)
+
+    def run(self, own, place_own, between, make_small):
+        count = self.pairs.shape[0]
+        eighth = count // 5
+        red = self.reduction
+        between = iter(between)
+        steps = gather(self.place, self.wires, own, self.near, self.far)
+        next(steps)
+        place_own()
+        next(between, None)
+        while next(steps) != "near":
+            next(between, None)
+        self.upper(0, 2 * eighth)
+        next(steps)
+        self.upper(2 * eighth, count)
+        self.collect(5, self.part_cols)
+        red.x[0].opposite()
+        red.x[1].opposite()
+        red.x[0].plain()
+        next(steps)
+        small = SmallSum(self.place, self.wires, self.slots).run(
+            make_small(energy(self.part_cols, self.far))
+        )
+        next(small)
+        self.lower(0, eighth)
+        red.x[0].joined()
+        red.x[2].opposite()
+        red.x[1].plain()
+        self.lower(eighth, 2 * eighth)
+        next(small)
+        red.x[1].joined()
+        red.x[3].opposite()
+        self.lower(2 * eighth, 3 * eighth)
+        red.x[2].plain()
+        next(small)
+        self.lower(3 * eighth, 4 * eighth)
+        red.x[2].joined()
+        red.x[3].plain()
+        self.lower(4 * eighth, count)
+        self.collect(4, self.part_rows)
+        red.cross_out()
+        next(small)
+        red.hold_x(0)
+        red.z.opposite()
+        for flip in (True, False):
+            red.cross_in(2, flip)
+            red.y[flip].opposite()
+        for flip in (True, False):
+            red.cross_in(1, flip)
+            red.cross_in(3, flip)
+            red.y[flip].plain()
+        red.x[3].joined()
+        next(small)
+        red.cross_in(0, True)
+        red.cross_in(0, False)
+        red.y[True].joined()
+        red.y[False].joined()
+        red.hold_x(1)
+        red.hold_x(2)
+        red.z.plain()
+        red.z.joined()
+        total = next(small)
+        red.hold_y(True)
+        red.zl_out()
+        red.hold_y(False)
+        red.hold_x(3)
+        return red.finish(), total
+
+
+def whole_kernel(total_rows, table, tiles, block, image_x, image_w, grams, *scratch):
+    (stage, stage_sems, pairs, sums, resid, send_sems, recv_sems), scratch = scratch[:7], scratch[7:]
+    sets = scratch[: len(scratch) // 2], scratch[len(scratch) // 2 :]
     place = Place()
     K, width = block.shape
     T = width // 2
-    greet(near_peers(place))
-    wires = Wires(place, send_sems, recv_sems)
-    steps = gather(place, wires, lambda u: block.at[:, pl.ds(u * T, T)], near, far)
-    next(steps)
-    for u in range(2):
-        half = block[:, u * T : (u + 1) * T]
-        near[place.col * 2 + u] = half
-        far[place.row * 2 + u] = half
-    next(steps)
-    wires.drain()
-
-
-def middle_kernel(
-    total_rows, block, near_x, part_rows, part_cols, image, rayleigh, grams, near, far, *scratch
-):
-    *boxes, slots, resid, send_sems, recv_sems = scratch
-    place = Place()
-    K, width = block.shape
-    T = width // 2
+    count = tiles.shape[0]
+    depth = stage.shape[0]
+
+    def fetch(s, slot):
+        return pltpu.make_async_copy(tiles.at[s], stage.at[slot], stage_sems.at[slot])
+
+    for s in range(depth):
+        fetch(s, s).start()
     greet(near_peers(place) + sum_peers(place))
     wires = Wires(place, send_sems, recv_sems)
-    small = SmallSum(place, wires, slots)
-    halves, total = reduce_all(
-        place, wires, small, part_rows, part_cols, boxes, lambda: fold(energy(part_rows, near_x))
+
+    def split_tiles(start, stop, more):
+        def step(s, carry):
+            slot = lax.rem(s, depth)
+            fetch(s, slot).wait()
+            pairs[s, 0], pairs[s, 1] = split(stage[slot])
+            if more:
+                fetch(s + depth, slot).start()
+            return carry
+
+        lax.fori_loop(start, stop, step, 0)
+
+    def prepare():
+        for start in range(0, count, depth):
+            split_tiles(start, start + depth, start + depth < count)
+            yield
+
+    def apply(number):
+        near, far, part_rows, part_cols, slots, *boxes = sets[number]
+        return Application(
+            place, wires, table, pairs, sums, near, far, part_rows, part_cols, boxes, slots
+        )
+
+    sums[0] = jnp.zeros((K, T), F32)
+    first = apply(0)
+
+    def place_block():
+        for u in range(2):
+            half = block[:, u * T : (u + 1) * T]
+            first.near[place.col * 2 + u] = half
+            first.far[place.row * 2 + u] = half
+
+    halves, total = first.run(
+        lambda u: block.at[:, pl.ds(u * T, T)], place_block, prepare(), fold
     )
     mean = unfold(total) / total_rows
     for u in range(2):
         resid[u] = halves[u] - dot_n(mean, block[:, u * T : (u + 1) * T], HIGHEST)
-    steps = gather(place, wires, lambda u: resid.at[u], near, far)
-    next(steps)
-    rayleigh[...] = mean
-    cross = jnp.zeros((K, K), F32)
-    square = jnp.zeros((K, K), F32)
+    second = apply(1)
+    local = {}
+
+    def place_resid():
+        grams[0] = mean
+        cross = jnp.zeros((K, K), F32)
+        square = jnp.zeros((K, K), F32)
+        for u in range(2):
+            image_x[:, u * T : (u + 1) * T] = halves[u]
+            value = resid[u]
+            second.near[place.col * 2 + u] = value
+            second.far[place.row * 2 + u] = value
+            cross += dot_t(halves[u], value, HIGHEST)
+            square += dot_t(value, value, HIGHEST)
+        grams[1] = cross
+        grams[3] = square
+
+    def make_small(middle):
+        return jnp.concatenate([fold(grams[1]), fold(middle), fold(grams[3])], axis=0)
+
+    halves, total = second.run(lambda u: resid.at[u], place_resid, (), make_small)
     for u in range(2):
-        image[:, u * T : (u + 1) * T] = halves[u]
-        value = resid[u]
-        near[place.col * 2 + u] = value
-        far[place.row * 2 + u] = value
-        cross += dot_t(halves[u], value, HIGHEST)
-        square += dot_t(value, value, HIGHEST)
-    grams[0] = cross
-    grams[1] = square
-    next(steps)
-    wires.drain()
-
-
-def last_kernel(
-    total_rows, rayleigh, local_grams, near_w, part_rows, part_cols, image, grams, *scratch
-):
-    *boxes, slots, send_sems, recv_sems = scratch
-    place = Place()
-    T = part_rows.shape[2]
-    half = rayleigh.shape[0] // 2
-    greet(near_peers(place) + sum_peers(place))
-    wires = Wires(place, send_sems, recv_sems)
-    small = SmallSum(place, wires, slots)
-
-    def make_small():
-        return jnp.concatenate(
-            [
-                fold(local_grams[0]),
-                fold(energy(part_rows, near_w)),
-                fold(local_grams[1]),
-            ],
-            axis=0,
-        )
-
-    halves, total = reduce_all(place, wires, small, part_rows, part_cols, boxes, make_small)
-    for u in range(2):
-        image[:, u * T : (u + 1) * T] = halves[u]
-    grams[0] = rayleigh[...]
+        image_w[:, u * T : (u + 1) * T] = halves[u]
+    half = K // 2
     for i in range(3):
         grams[1 + i] = unfold(total[i * half : (i + 1) * half]) / total_rows
     wires.drain()
 
 
-def tile_kernel(
-    count, row_ids, col_ids, tiles, near, far, part_rows, part_cols, held, near_two, far_two, sems
-):
-    slots = tiles.shape[0]
+def table_kernel(count, row_ids, col_ids, table):
     live = count[0]
-
-    def fetch(s):
-        return pltpu.make_async_copy(tiles.at[s], held.at[s], sems.at[s])
-
-    for s in range(slots):
-        fetch(s).start()
-    zero = jnp.zeros(part_rows.shape[1:], F32)
-
-    def prepare(p, carry):
-        part_rows[p] = zero
-        part_cols[p] = zero
-        near_two[p] = jnp.concatenate(split(near[p]), axis=0)
-        far_two[p] = jnp.concatenate(split(far[p]), axis=0)
+    slots = row_ids.shape[0]
+
+    def clear(s, carry):
+        for line in range(2, 6):
+            table[line, s] = 0
         return carry
 
-    lax.fori_loop(0, part_rows.shape[0], prepare, 0)
-    K = near.shape[1]
+    lax.fori_loop(0, slots, clear, 0)
 
     def step(s, carry):
-        fetch(s).wait()
         row, col = row_ids[s], col_ids[s]
-        high, low = split(held[s])
-        rows_in, cols_in = near_two[row], far_two[col]
-        lower = dot_t(cols_in, high)
-        upper = dot_n(rows_in, high)
-        part_rows[row] += (lower[:K] + lower[K:]) + dot_t(cols_in[:K], low)
-        part_cols[col] += (upper[:K] + upper[K:]) + dot_n(rows_in[:K], low)
+        table[0, s] = row
+        table[1, s] = col
+        alive = s < live
+        for line, at in ((4, row), (5, col)):
+            before = table[line, at]
+            table[line - 2, s] = jnp.where(alive, before, 0)
+            table[line, at] = jnp.where(alive, s + 1, before)
         return carry
 
-    lax.fori_loop(0, live, step, 0)
-
-    def finish(s, carry):
-        fetch(s).wait()
-        return carry
-
-    lax.fori_loop(live, slots, finish, 0)
+    lax.fori_loop(0, slots, step, 0)
 
 
 def vmem(count):
@@ -584,73 +665,41 @@
     T = tiles.shape[-1]
     slots = tiles.shape[2]
     total_rows = width * lax.axis_size("row") * lax.axis_size("col")
-    count, row_ids, col_ids = tile_count[0], tile_rows[0, 0], tile_cols[0, 0]
-    data = tiles[0, 0]
-    strip = jax.ShapeDtypeStruct((32, K, T), F32)
+    smem = pl.BlockSpec(memory_space=pltpu.SMEM)
+    table = pl.pallas_call(
+        table_kernel,
+        out_shape=jax.ShapeDtypeStruct((6, slots), jnp.int32),
+        in_specs=[smem] * 3,
+        out_specs=smem,
+        name="slot_table",
+    )(tile_count[0], tile_rows[0, 0], tile_cols[0, 0])
+    strip = pltpu.VMEM((32, K, T), F32)
     seg = jax.ShapeDtypeStruct((K, width), F32)
 
-    def params(number):
-        return pltpu.CompilerParams(
-            collective_id=number, has_side_effects=True, vmem_limit_bytes=VMEM_LIMIT
-        )
-
-    def sems(count):
-        return [pltpu.SemaphoreType.DMA((count,)), pltpu.SemaphoreType.DMA((count,))]
-
-    near, far = pl.pallas_call(
-        first_kernel,
-        out_shape=(strip, strip),
-        in_specs=vmem(1),
-        out_specs=tuple(vmem(2)),
-        scratch_shapes=sems(60),
-        compiler_params=params(0),
-        name="gather_block",
-    )(block)
-
-    def products(near, far):
-        smem = pl.BlockSpec(memory_space=pltpu.SMEM)
-        return pl.pallas_call(
-            tile_kernel,
-            out_shape=(strip, strip),
-            in_specs=[smem, smem, smem, pl.BlockSpec(memory_space=pl.ANY)] + vmem(2),
-            out_specs=tuple(vmem(2)),
-            scratch_shapes=[
-                pltpu.VMEM((slots, T, T), F32),
-                pltpu.VMEM((32, 2 * K, T), BF16),
-                pltpu.VMEM((32, 2 * K, T), BF16),
-                pltpu.SemaphoreType.DMA((slots,)),
-            ],
-            compiler_params=pltpu.CompilerParams(vmem_limit_bytes=VMEM_LIMIT),
-            name="tile_products",
-        )(count, row_ids, col_ids, data, near, far)
-
-    part_rows, part_cols = products(near, far)
-    image_x, rayleigh, local_grams, near_w, far_w = pl.pallas_call(
-        functools.partial(middle_kernel, total_rows),
-        out_shape=(
-            seg,
-            jax.ShapeDtypeStruct((K, K), F32),
-            jax.ShapeDtypeStruct((2, K, K), F32),
-            strip,
-            strip,
+    def one_set(rows):
+        return [strip] * 4 + [pltpu.VMEM((5, 4, rows, 2 * K), F32)] + reduce_scratch(K, T)
+
+    return pl.pallas_call(
+        functools.partial(whole_kernel, total_rows),
+        out_shape=(seg, seg, jax.ShapeDtypeStruct((4, K, K), F32)),
+        in_specs=[smem, pl.BlockSpec(memory_space=pl.ANY)] + vmem(1),
+        out_specs=tuple(vmem(3)),
+        scratch_shapes=[
+            pltpu.VMEM((8, T, T), F32),
+            pltpu.SemaphoreType.DMA((8,)),
+            pltpu.VMEM((slots, 2, T, T), BF16),
+            pltpu.VMEM((slots + 1, K, T), F32),
+            pltpu.VMEM((2, K, T), F32),
+            pltpu.SemaphoreType.DMA((280,)),
+            pltpu.SemaphoreType.DMA((280,)),
+        ]
+        + one_set(K // 2)
+        + one_set(3 * K // 2),
+        compiler_params=pltpu.CompilerParams(
+            collective_id=0, has_side_effects=True, vmem_limit_bytes=VMEM_LIMIT
         ),
-        in_specs=vmem(4),
-        out_specs=tuple(vmem(5)),
-        scratch_shapes=reduce_scratch(K, T, K // 2) + [pltpu.VMEM((2, K, T), F32)] + sems(136),
-        compiler_params=params(1),
-        name="reduce_and_gather",
-    )(block, near, part_rows, part_cols)
-    part_rows, part_cols = products(near_w, far_w)
-    image_w, grams = pl.pallas_call(
-        functools.partial(last_kernel, total_rows),
-        out_shape=(seg, jax.ShapeDtypeStruct((4, K, K), F32)),
-        in_specs=vmem(5),
-        out_specs=tuple(vmem(2)),
-        scratch_shapes=reduce_scratch(K, T, 3 * K // 2) + sems(76),
-        compiler_params=params(2),
-        name="reduce_last",
-    )(rayleigh, local_grams, near_w, part_rows, part_cols)
-    return image_x, image_w, grams
+        name="rayleigh_ritz",
+    )(table, tiles[0, 0], block)
 
 
 def solution(mesh):

time: 172 us -> 152 us (0.88)
  Pallas kernels: 168 us -> 146 us
    pallas_call x5 -> x2, Pallas kernels: 168 us -> 146 us  [the longest x1 144 us: on_device(): pl.pallas_call(functools.partial(whole_kernel, total_rows), out_shape=(se...]
    unnamed x5 -> x3, local copies, waits for them, and re-layouts: 3.8 us -> 4.7 us
where the time goes in v2:
time: 152 us
  Pallas kernels  146 us (96%)
  local copies, waits for them, and re-layouts  4.7 us (3%)
    pallas_call x1, Pallas kernels, on_device(): pl.pallas_call(functools.partial(whole_kernel, total_rows), out_shape=(se...  144 us
    unnamed x3, local copies, waits for them, and re-layouts  4.7 us

profile of v2, /device:TPU:1, one launch (start us, length us, event | category | flops | bytes accessed | tf_op | source)
XLA Modules:
  0.0 151.8 jit_solution(4625929483831632793)
XLA Ops:
  1.3 2.2 %slot_table.1.table = s32[6,40]{1,0:T(8,128)} custom-call(s32[1]{0:T(128)} %bitcast.4.count, s32[40]{0:T(128)} %bitcast.6, s32[40]{0:T(128)} %bitcast.7), custom_call_target="tpu_custom_call" | custom-call | tf_op jit(solution)/shard_map/slot_table/pallas_call | solution.py:669
  3.5 143.7 %rayleigh_ritz.1 = (f32[64,512]{1,0:T(8,128)}, f32[64,512]{1,0:T(8,128)}, f32[4,64,64]{2,1,0:T(8,128)}) custom-call(s32[6,40]{1,0:T(8,128)} %slot_table.1.table, f32[40,256,256]{2,1,0:T(8,128)} %bitcast.5, f32[64,512]{1,0:T(8,128)} %block.1), custom_call_target="tpu_custom_call" | custom-call | tf_op jit(solution)/shard_map/rayleigh_ritz/pallas_call | solution.py:682
  147.1 1.6 %copy.12 = f32[64,512]{1,0:T(8,128)} copy(f32[64,512]{1,0:T(8,128)} %get-tuple-element.6) | data formatting | bytes 262144
  148.7 1.6 %copy.13 = f32[64,512]{1,0:T(8,128)} copy(f32[64,512]{1,0:T(8,128)} %get-tuple-element.7) | data formatting | bytes 262144
  150.3 1.6 %copy.14 = f32[4,64,64]{2,1,0:T(8,128)} copy(f32[4,64,64]{2,1,0:T(8,128)} %get-tuple-element.8) | data formatting | bytes 131072

commit v3 on v2

v3 whole, which is shorter than its diff:
```python
import functools

import jax
import jax.numpy as jnp
from jax import lax
from jax.experimental import pallas as pl
from jax.experimental.pallas import tpu as pltpu
from jax.sharding import PartitionSpec as P

MESH = pl.DeviceIdType.MESH
HIGHEST = lax.Precision.HIGHEST
F32 = jnp.float32
BF16 = jnp.bfloat16
RING = 4
VMEM_LIMIT = 60 * 1024 * 1024
UNROLL = 8
CHUNKS = 5
PREPARE = 4
STAGE = 16
(
    KSTART, KOWN, KZL, KZP, KZM, KZO, KXA, KXB, KYP, KYM, KYO, KNEAR, KFAR, KP, KU, KCOLS, KL,
    KROWS, KOP, KOM, KPP, KPM, KRL, KRH, KTA, KTB, KCO, KCI, KQO, KQM, KQP, KQN, KQL, KQH, KQA, KQB,
    KWO, KWQ, KWP, KWM, KWL, KWH, KE, KS, KT,
) = range(45)
(
    TO_XP, TO_XM, TO_YP, TO_YM, TO_CORE, TO_ZP, TO_ZM, TO_ZL, FZP, FZM, FXP, FXM, FYP, FYM,
) = range(14)
(
    DZ, DL, DX, DY,
) = range(4)
START = (
    (DZ, 0), (DL, 0), (DX, 0), (DY, 0), (DL, 1), (DZ, 1), (DX, 1), (DY, 1),
)
SUM_ORDER = (0, 4, 1, 3, 2)
EARLY_ORDER = (3, 1, 4, 2, 0)
FIRST_ORDER = (
    0, 31, 32, 33, 34, 9, 17, 18, 35, 36, 10, 2, 20, 21, 7, 1, 37, 19, 5, 38, 3, 39, 11, 22, 40, 6, 23, 24, 41,
    14, 8, 26, 27, 13, 4, 25, 12, 28, 29, 16, 42, 43, 44, 15, 45, 46, 47, 54, 55, 63, 70, 56, 57, 62, 71, 30,
    48, 119, 58, 74, 59, 67, 49, 64, 120, 73, 50, 51, 65, 72, 52, 66, 53, 86, 75, 60, 111, 61, 112, 87, 91, 80,
    99, 81, 92, 88, 93, 100, 89, 78, 101, 79, 121, 69, 113, 90, 94, 102, 76, 114, 103, 104, 95, 96, 68, 77, 122,
    115, 105, 116, 106, 107, 82, 83, 108, 97, 98, 123, 109, 84, 85, 110, 117, 124, 118,
)
SECOND_ORDER = (
    0, 31, 115, 9, 17, 18, 10, 20, 21, 2, 7, 1, 116, 19, 5, 3, 22, 11, 23, 24, 6, 26, 14, 8, 27, 13, 117, 4, 25,
    12, 28, 29, 32, 16, 33, 34, 15, 35, 36, 37, 44, 45, 53, 60, 118, 46, 47, 52, 61, 30, 38, 109, 48, 64, 49,
    57, 39, 54, 110, 63, 40, 41, 55, 62, 42, 56, 43, 76, 65, 119, 50, 101, 51, 102, 77, 81, 70, 89, 71, 82, 78,
    83, 90, 79, 68, 91, 69, 111, 59, 103, 80, 84, 92, 66, 104, 93, 120, 94, 85, 86, 58, 67, 112, 105, 95, 106,
    96, 97, 72, 73, 98, 87, 88, 113, 99, 74, 75, 100, 107, 114, 108,
)


class Place:
    def __init__(self):
        row = lax.axis_index("row")
        col = lax.axis_index("col")
        self.x, self.zh = lax.div(row, RING), lax.rem(row, RING)
        self.y = lax.div(col, RING)
        rest = lax.rem(col, RING)
        self.zl, self.core = lax.div(rest, 2), lax.rem(rest, 2)
        self.row, self.col = row, col

    def turn(self, value, by):
        return lax.rem(value + by, RING)

    def row_at(self, dx=0, dz=0):
        return self.turn(self.x, dx) * RING + self.turn(self.zh, dz)

    def col_at(self, dy=0, flip_zl=False, flip_core=False):
        zl = 1 - self.zl if flip_zl else self.zl
        core = 1 - self.core if flip_core else self.core
        return (self.turn(self.y, dy) * 2 + zl) * 2 + core

    def peer(self, dx=0, dz=0, dy=0, flip_zl=False, flip_core=False):
        return (self.row_at(dx, dz), self.col_at(dy, flip_zl, flip_core))


class Wires:
    def __init__(self, place, send_sems, recv_sems):
        self.place, self.send_sems, self.recv_sems = place, send_sems, recv_sems
        self.sent = []

    def send(self, src, dst, peer):
        number = len(self.sent)
        copy = pltpu.make_async_remote_copy(
            src_ref=src,
            dst_ref=dst,
            send_sem=self.send_sems.at[number],
            recv_sem=self.recv_sems.at[number],
            device_id=peer,
            device_id_type=MESH,
        )
        copy.start()
        self.sent.append(copy)
        return number

    def arrived(self, number, landing):
        pltpu.make_async_remote_copy(
            src_ref=landing,
            dst_ref=landing,
            send_sem=self.send_sems.at[number],
            recv_sem=self.recv_sems.at[number],
            device_id=self.place.peer(flip_core=True),
            device_id_type=MESH,
        ).wait_recv()

    def drain(self):
        for copy in self.sent:
            copy.wait_send()


def greet(peers):
    barrier = pltpu.get_barrier_semaphore()
    for peer in peers:
        pl.semaphore_signal(barrier, inc=1, device_id=peer, device_id_type=MESH)
    pl.semaphore_wait(barrier, len(peers))


def near_peers(place):
    return [
        place.peer(dx=1),
        place.peer(dx=3),
        place.peer(dz=1),
        place.peer(dz=3),
        place.peer(dy=1),
        place.peer(dy=3),
        place.peer(flip_zl=True),
        place.peer(flip_core=True),
    ]


def sum_peers(place):
    return [place.peer(dx=2), place.peer(dz=2), place.peer(dy=2)]


class Step:
    def __init__(self, before, waits, act):
        self.before, self.waits, self.act = before, waits, act

    def run(self, wires):
        for number, landing in self.waits():
            wires.arrived(number, landing)
        self.act()


def nothing():
    return ()


def gather_steps(place, wires, own, near, far, steps):
    send = wires.send

    def far_at(u, dx=0, dz=0):
        return far.at[place.row_at(dx, dz) * 2 + u]

    def near_at(u, dy=0, flip_zl=False, flip_core=False):
        return near.at[place.col_at(dy, flip_zl, flip_core) * 2 + u]

    xp, xm = place.peer(dx=1), place.peer(dx=3)
    zp, zm = place.peer(dz=1), place.peer(dz=3)
    yp, ym = place.peer(dy=1), place.peer(dy=3)
    zl_peer, core_peer = place.peer(flip_zl=True), place.peer(flip_core=True)
    sent = {}

    def x_out(dz, u, src):
        sent[TO_XP, dz, u] = send(src, far_at(u, dz=dz), xp)
        sent[TO_XM, dz, u] = send(src, far_at(u, dz=dz), xm)

    def y_out(flip, u, src):
        sent[TO_YP, flip, u] = send(src, near_at(u, flip_zl=flip), yp)
        sent[TO_YM, flip, u] = send(src, near_at(u, flip_zl=flip), ym)

    def share(dy, flip, u, src):
        sent[TO_CORE, dy, flip, u] = send(src, near_at(u, dy, flip), core_peer)

    def start():
        for name, u in START:
            if name == DZ:
                sent[TO_ZP, u] = send(own(u), far_at(u), zp)
                sent[TO_ZM, 1 - u] = send(own(1 - u), far_at(1 - u), zm)
            elif name == DL:
                sent[TO_ZL, u] = send(own(u), near_at(u), zl_peer)
            elif name == DX:
                x_out(0, u, own(u))
            else:
                y_out(False, u, own(u))
        for u in range(2):
            share(0, False, u, own(u))

    steps[(KSTART,)] = Step((), nothing, start)

    def add(name, key, landing, act, before=((KSTART,),)):
        steps[name] = Step(before, lambda: [(sent[key], landing)], act)

    for u in range(2):

        def zl_in(u=u):
            y_out(True, u, near_at(u, flip_zl=True))
            share(0, True, u, near_at(u, flip_zl=True))

        add((KZL, u), (TO_ZL, u), near_at(u, flip_zl=True), zl_in)

        def zp_in(u=u):
            if u == 0:
                sent[FZP] = send(far_at(0, dz=3), far_at(0, dz=3), zp)
            x_out(3, u, far_at(u, dz=3))

        def zm_in(u=u):
            if u == 1:
                sent[FZM] = send(far_at(1, dz=1), far_at(1, dz=1), zm)
            x_out(1, u, far_at(u, dz=1))

        add((KZP, u), (TO_ZP, u), far_at(u, dz=3), zp_in)
        add((KZM, u), (TO_ZM, u), far_at(u, dz=1), zm_in)
        key, before = (FZP, (KZP, 0)) if u == 0 else (FZM, (KZM, 1))
        add(
            (KZO, u),
            key,
            far_at(u, dz=2),
            lambda u=u: x_out(2, u, far_at(u, dz=2)),
            (before,),
        )
    origins = {
        0: ((KSTART,), (KSTART,)),
        3: ((KZP, 0), (KZP, 1)),
        1: ((KZM, 0), (KZM, 1)),
        2: ((KZO, 0), (KZO, 1)),
    }
    for dz in (0, 3, 1, 2):

        def plus_in(dz=dz):
            sent[FXP, dz] = send(far_at(0, dx=3, dz=dz), far_at(0, dx=3, dz=dz), xp)

        def minus_in(dz=dz):
            sent[FXM, dz] = send(far_at(1, dx=1, dz=dz), far_at(1, dx=1, dz=dz), xm)

        add((KXA, dz), (TO_XP, dz, 0), far_at(0, dx=3, dz=dz), plus_in, (origins[dz][0],))
        add((KXB, dz), (TO_XM, dz, 1), far_at(1, dx=1, dz=dz), minus_in, (origins[dz][1],))
    for flip in (False, True):
        for u in range(2):
            before = ((KZL, u),) if flip else ((KSTART,),)

            def plus_y(flip=flip, u=u):
                if u == 0:
                    sent[FYP, flip] = send(near_at(0, 3, flip), near_at(0, 3, flip), yp)
                share(3, flip, u, near_at(u, 3, flip))

            def minus_y(flip=flip, u=u):
                if u == 1:
                    sent[FYM, flip] = send(near_at(1, 1, flip), near_at(1, 1, flip), ym)
                share(1, flip, u, near_at(u, 1, flip))

            add((KYP, int(flip), u), (TO_YP, flip, u), near_at(u, 3, flip), plus_y, before)
            add((KYM, int(flip), u), (TO_YM, flip, u), near_at(u, 1, flip), minus_y, before)
            key, origin = (FYP, KYP) if u == 0 else (FYM, KYM)
            add(
                (KYO, int(flip), u),
                (key, flip),
                near_at(u, 2, flip),
                lambda flip=flip, u=u: share(2, flip, u, near_at(u, 2, flip)),
                ((origin, int(flip), u),),
            )

    def near_waits():
        return [
            (sent[TO_CORE, dy, flip, u], near_at(u, dy, flip, True))
            for flip in (False, True)
            for dy in (0, 1, 3, 2)
            for u in range(2)
        ]

    def far_waits():
        waits = []
        for dz in (0, 3, 1, 2):
            waits.append((sent[TO_XM, dz, 0], far_at(0, dx=1, dz=dz)))
            waits.append((sent[TO_XP, dz, 1], far_at(1, dx=3, dz=dz)))
            waits.append((sent[FXP, dz], far_at(0, dx=2, dz=dz)))
            waits.append((sent[FXM, dz], far_at(1, dx=2, dz=dz)))
        return waits

    y_names = tuple(n for n in steps if n[0] in (KZL, KYP, KYM, KYO))
    x_names = tuple(n for n in steps if n[0] in (KZP, KZM, KZO, KXA, KXB))
    steps[(KNEAR,)] = Step(((KOWN,),) + y_names, near_waits, lambda: None)
    steps[(KFAR,)] = Step(((KOWN,),) + x_names, far_waits, lambda: None)


class RingSum:
    def __init__(self, wires, term, box, pair, plus, minus):
        self.wires, self.term, self.box, self.pair = wires, term, box, pair
        self.plus, self.minus = plus, minus

    def opposite_plus(self):
        self.opp_plus = self.wires.send(self.term(2, 0), self.box(0), self.plus)

    def opposite_minus(self):
        self.opp_minus = self.wires.send(self.term(2, 1), self.box(1), self.minus)

    def plain_plus(self):
        self.plus_sent = self.wires.send(self.term(1, 1), self.box(2), self.plus)

    def plain_minus(self):
        self.minus_sent = self.wires.send(self.term(3, 0), self.box(3), self.minus)

    def low_waits(self):
        return [(self.opp_plus, self.box(0))]

    def join_low(self):
        self.pair(0)[...] = self.term(1, 0)[...] + self.box(0)[...]
        self.low_sent = self.wires.send(self.pair(0), self.box(4), self.plus)

    def high_waits(self):
        return [(self.opp_minus, self.box(1))]

    def join_high(self):
        self.pair(1)[...] = self.term(3, 1)[...] + self.box(1)[...]
        self.high_sent = self.wires.send(self.pair(1), self.box(5), self.minus)

    def low_total_waits(self):
        return [(self.minus_sent, self.box(3)), (self.low_sent, self.box(4))]

    def high_total_waits(self):
        return [(self.plus_sent, self.box(2)), (self.high_sent, self.box(5))]

    def low_total(self):
        return self.term(0, 0)[...] + (self.box(4)[...] + self.box(3)[...])

    def high_total(self):
        return self.term(0, 1)[...] + (self.box(2)[...] + self.box(5)[...])


class SmallSum:
    def __init__(self, place, wires, slots):
        self.place, self.wires, self.slots = place, wires, slots

    def pair_out(self, stage, value, mine, peer):
        self.mine = mine
        self.slots[stage, mine] = value
        self.numbers = [self.wires.send(self.slots.at[stage, mine], self.slots.at[stage, mine], peer)]

    def pair_waits(self, stage):
        return [(self.numbers[0], self.slots.at[stage, 1 - self.mine])]

    def pair_in(self, stage):
        return self.slots[stage, 0] + self.slots[stage, 1]

    def ring_out(self, stage, value, mine, peers):
        self.mine = mine
        self.slots[stage, mine] = value
        self.numbers = [
            self.wires.send(self.slots.at[stage, mine], self.slots.at[stage, mine], peers[by])
            for by in (1, 2, 3)
        ]

    def ring_waits(self, stage):
        return [
            (number, self.slots.at[stage, lax.rem(self.mine + RING - by, RING)])
            for number, by in zip(self.numbers, (1, 2, 3))
        ]

    def ring_in(self, stage):
        return (self.slots[stage, 0] + self.slots[stage, 1]) + (self.slots[stage, 2] + self.slots[stage, 3])

    def add_steps(self, steps, kind, order, make_value, before):
        place = self.place
        places = (place.core, place.zl, place.y, place.x, place.zh)

        def out(stage, value):
            axis = order[stage]
            if axis == 0:
                self.pair_out(stage, value, places[axis], place.peer(flip_core=True))
            elif axis == 1:
                self.pair_out(stage, value, places[axis], place.peer(flip_zl=True))
            elif axis == 2:
                self.ring_out(stage, value, places[axis], {by: place.peer(dy=by) for by in (1, 2, 3)})
            elif axis == 3:
                self.ring_out(stage, value, places[axis], {by: place.peer(dx=by) for by in (1, 2, 3)})
            else:
                self.ring_out(stage, value, places[axis], {by: place.peer(dz=by) for by in (1, 2, 3)})

        def waits(stage):
            return self.pair_waits(stage) if order[stage] < 2 else self.ring_waits(stage)

        def take(stage):
            return self.pair_in(stage) if order[stage] < 2 else self.ring_in(stage)

        def last():
            self.result = take(4)

        steps[(kind, 0)] = Step(before, nothing, lambda: out(0, make_value()))
        for stage in range(1, 5):
            steps[(kind, stage)] = Step(
                ((kind, stage - 1),),
                functools.partial(waits, stage - 1),
                lambda stage=stage: out(stage, take(stage - 1)),
            )
        steps[(kind, 5)] = Step(((kind, 4),), functools.partial(waits, 4), last)


class Reduction:
    depths = (2, 1, 3, 0)

    def __init__(self, place, wires, part_rows, part_cols, boxes):
        self.place, self.wires = place, wires
        self.part_rows = part_rows
        (
            self.core_box,
            self.near_sum,
            y_box,
            y_pair,
            self.y_held,
            self.zl_box,
            x_box,
            x_pair,
            self.x_held,
            z_box,
            z_pair,
        ) = boxes
        xp, xm = place.peer(dx=1), place.peer(dx=3)
        zp, zm = place.peer(dz=1), place.peer(dz=3)
        yp, ym = place.peer(dy=1), place.peer(dy=3)
        self.zl_peer = place.peer(flip_zl=True)
        self.core_peer = place.peer(flip_core=True)

        def x_ring(k, dz):
            return RingSum(
                wires,
                lambda d, u: part_cols.at[place.row_at(d, dz) * 2 + u],
                lambda i: x_box.at[k, i],
                lambda i: x_pair.at[k, i],
                xp,
                xm,
            )

        def y_ring(flip):
            return RingSum(
                wires,
                lambda d, u: self.near_sum.at[d, int(flip), u],
                lambda i: y_box.at[int(flip), i],
                lambda i: y_pair.at[int(flip), i],
                yp,
                ym,
            )

        self.x = [x_ring(k, dz) for k, dz in enumerate(self.depths)]
        self.y = {flip: y_ring(flip) for flip in (True, False)}
        self.z = RingSum(
            wires,
            lambda d, u: self.x_held.at[self.depths.index(d), u],
            lambda i: z_box.at[i],
            lambda i: z_pair.at[i],
            zp,
            zm,
        )

    def cross_out(self):
        self.crossed = {}
        for dy in (2, 1, 3, 0):
            for flip in (True, False):
                source = self.place.col_at(dy, flip, True) * 2
                self.crossed[dy, flip] = self.wires.send(
                    self.part_rows.at[pl.ds(source, 2)],
                    self.core_box.at[dy, int(flip)],
                    self.core_peer,
                )

    def cross_waits(self, dy, flip):
        return [(self.crossed[dy, flip], self.core_box.at[dy, int(flip)])]

    def cross_in(self, dy, flip):
        source = self.place.col_at(dy, flip) * 2
        self.near_sum[dy, int(flip)] = self.part_rows[pl.ds(source, 2)] + self.core_box[dy, int(flip)]

    def low_x(self, k):
        self.x_held[k, 0] = self.x[k].low_total()

    def high_x(self, k):
        self.x_held[k, 1] = self.x[k].high_total()

    def low_y(self, flip):
        self.y_held[int(flip), 0] = self.y[flip].low_total()
        self.zl_share(flip, 0)

    def high_y(self, flip):
        self.y_held[int(flip), 1] = self.y[flip].high_total()
        self.zl_share(flip, 1)

    def zl_share(self, flip, u):
        if flip:
            self.zl_sent[u] = self.wires.send(self.y_held.at[1, u], self.zl_box.at[u], self.zl_peer)

    def finish(self, u):
        total = self.z.high_total() if u else self.z.low_total()
        self.result[u] = total + (self.y_held[0, u] + self.zl_box[u])

    def add_steps(self, steps):
        self.zl_sent, self.result = {}, {}
        for k, ring in enumerate(self.x):
            steps[(KOP, k)] = Step(((KCOLS,),), nothing, ring.opposite_plus)
            steps[(KOM, k)] = Step(((KCOLS,),), nothing, ring.opposite_minus)
            steps[(KPP, k)] = Step(((KCOLS,),), nothing, ring.plain_plus)
            steps[(KPM, k)] = Step(((KCOLS,),), nothing, ring.plain_minus)
            steps[(KRL, k)] = Step(((KOP, k),), ring.low_waits, ring.join_low)
            steps[(KRH, k)] = Step(((KOM, k),), ring.high_waits, ring.join_high)
            steps[(KTA, k)] = Step(
                ((KRL, k), (KPM, k)), ring.low_total_waits, functools.partial(self.low_x, k)
            )
            steps[(KTB, k)] = Step(
                ((KRH, k), (KPP, k)), ring.high_total_waits, functools.partial(self.high_x, k)
            )
        steps[(KCO,)] = Step(((KROWS,),), nothing, self.cross_out)
        for flip in (True, False):
            f = int(flip)
            ring = self.y[flip]
            for dy in (2, 1, 3, 0):
                steps[(KCI, dy, f)] = Step(
                    ((KCO,),),
                    functools.partial(self.cross_waits, dy, flip),
                    functools.partial(self.cross_in, dy, flip),
                )
            steps[(KQO, f)] = Step(((KCI, 2, f),), nothing, ring.opposite_plus)
            steps[(KQM, f)] = Step(((KCI, 2, f),), nothing, ring.opposite_minus)
            steps[(KQP, f)] = Step(((KCI, 1, f),), nothing, ring.plain_plus)
            steps[(KQN, f)] = Step(((KCI, 3, f),), nothing, ring.plain_minus)
            steps[(KQL, f)] = Step(((KQO, f), (KCI, 1, f)), ring.low_waits, ring.join_low)
            steps[(KQH, f)] = Step(((KQM, f), (KCI, 3, f)), ring.high_waits, ring.join_high)
            steps[(KQA, f)] = Step(
                ((KQL, f), (KQN, f), (KCI, 0, f)),
                ring.low_total_waits,
                functools.partial(self.low_y, flip),
            )
            steps[(KQB, f)] = Step(
                ((KQH, f), (KQP, f), (KCI, 0, f)),
                ring.high_total_waits,
                functools.partial(self.high_y, flip),
            )
        steps[(KWO,)] = Step(((KTA, 0),), nothing, self.z.opposite_plus)
        steps[(KWQ,)] = Step(((KTB, 0),), nothing, self.z.opposite_minus)
        steps[(KWP,)] = Step(((KTB, 1),), nothing, self.z.plain_plus)
        steps[(KWM,)] = Step(((KTA, 2),), nothing, self.z.plain_minus)
        steps[(KWL,)] = Step(((KWO,), (KTA, 1)), self.z.low_waits, self.z.join_low)
        steps[(KWH,)] = Step(((KWQ,), (KTB, 2)), self.z.high_waits, self.z.join_high)
        steps[(KE, 0)] = Step(
            ((KWM,), (KWL,), (KTA, 3), (KQA, 0), (KQA, 1)),
            lambda: [(self.zl_sent[0], self.zl_box.at[0])] + self.z.low_total_waits(),
            lambda: self.finish(0),
        )
        steps[(KE, 1)] = Step(
            ((KWP,), (KWH,), (KTB, 3), (KQB, 0), (KQB, 1)),
            lambda: [(self.zl_sent[1], self.zl_box.at[1])] + self.z.high_total_waits(),
            lambda: self.finish(1),
        )


def reduce_scratch(K, T):
    return [
        pltpu.VMEM((4, 2, 2, K, T), F32),
        pltpu.VMEM((4, 2, 2, K, T), F32),
        pltpu.VMEM((2, 6, K, T), F32),
        pltpu.VMEM((2, 2, K, T), F32),
        pltpu.VMEM((2, 2, K, T), F32),
        pltpu.VMEM((2, K, T), F32),
        pltpu.VMEM((4, 6, K, T), F32),
        pltpu.VMEM((4, 2, K, T), F32),
        pltpu.VMEM((4, 2, K, T), F32),
        pltpu.VMEM((6, K, T), F32),
        pltpu.VMEM((2, K, T), F32),
    ]


def split(value):
    high = value.astype(BF16)
    low = (value - high.astype(F32)).astype(BF16)
    return high, low


def dot_t(left, right, precision=None):
    return lax.dot_general(
        left, right, (((1,), (1,)), ((), ())), precision=precision, preferred_element_type=F32
    )


def dot_n(left, right, precision=None):
    return lax.dot_general(
        left, right, (((1,), (0,)), ((), ())), precision=precision, preferred_element_type=F32
    )


def fold(square):
    half = square.shape[0] // 2
    return jnp.concatenate([square[:half], square[half:]], axis=1)


def unfold(flat):
    half = flat.shape[1] // 2
    return jnp.concatenate([flat[:, :half], flat[:, half:]], axis=0)


def energy(part, vectors):
    K = part.shape[1]
    group = 4

    def step(g, total):
        left = [jnp.concatenate(split(part[g * group + i]), axis=0) for i in range(group)]
        right = [jnp.concatenate(split(vectors[g * group + i]), axis=0) for i in range(group)]
        return total + dot_t(jnp.concatenate(left, axis=1), jnp.concatenate(right, axis=1))

    total = lax.fori_loop(0, part.shape[0] // group, step, jnp.zeros((2 * K, 2 * K), F32))
    total = total[:K] + total[K:]
    total = total[:, :K] + total[:, K:]
    return total + total.T


class Application:
    def __init__(
        self, place, wires, table, pairs, sums, near, far, part_rows, part_cols, boxes, slots, early_slots
    ):
        self.place, self.wires, self.table, self.pairs, self.sums = place, wires, table, pairs, sums
        self.near, self.far = near, far
        self.part_rows, self.part_cols = part_rows, part_cols
        self.slots, self.early_slots = slots, early_slots
        self.reduction = Reduction(place, wires, part_rows, part_cols, boxes)

    def products(self, vectors, ids, before, transposed, start, stop):
        K = self.near.shape[1]
        dot = dot_t if transposed else dot_n

        def product(s):
            high, low = split(vectors[self.table[ids, s]])
            both = dot(jnp.concatenate([high, low], axis=0), self.pairs[s, 0])
            return (both[:K] + both[K:]) + dot(high, self.pairs[s, 1])

        def step(group, carry):
            slots = [group * UNROLL + i for i in range(UNROLL)]
            for s, value in zip(slots, [product(s) for s in slots]):
                self.sums[s + 1] = value + self.sums[self.table[before, s]]
            return carry

        lax.fori_loop(start // UNROLL, stop // UNROLL, step, 0)

    def upper(self, start, stop):
        self.products(self.near, 0, 3, False, start, stop)

    def lower(self, start, stop):
        self.products(self.far, 1, 2, True, start, stop)

    def collect(self, line, parts):
        def step(group, carry):
            for i in range(4):
                p = group * 4 + i
                parts[p] = self.sums[self.table[line, p]]
            return carry

        lax.fori_loop(0, parts.shape[0] // 4, step, 0)

    def steps(self, own, place_own, prepare, early):
        steps = {}
        gather_steps(self.place, self.wires, own, self.near, self.far, steps)
        steps[(KOWN,)] = Step(((KSTART,),), nothing, place_own)
        ready = ()
        for i, chunk in enumerate(prepare):
            steps[(KP, i)] = Step(ready, nothing, chunk)
            ready = ((KP, i),)
        last = ((KNEAR,),) + ready
        for i in range(CHUNKS):
            size = self.pairs.shape[0] // CHUNKS
            act = functools.partial(self.upper, i * size, (i + 1) * size)
            steps[(KU, i)] = Step(last, nothing, act)
            last = ((KU, i),)
        steps[(KCOLS,)] = Step(last, nothing, lambda: self.collect(5, self.part_cols))
        last = ((KFAR,), (KCOLS,))
        for i in range(CHUNKS):
            act = functools.partial(self.lower, i * size, (i + 1) * size)
            steps[(KL, i)] = Step(last, nothing, act)
            last = ((KL, i),)
        steps[(KROWS,)] = Step(last, nothing, lambda: self.collect(4, self.part_rows))
        self.reduction.add_steps(steps)
        self.small = SmallSum(self.place, self.wires, self.slots)
        self.early = SmallSum(self.place, self.wires, self.early_slots)
        self.small.add_steps(
            steps,
            KS,
            SUM_ORDER,
            lambda: fold(energy(self.part_cols, self.far)),
            ((KFAR,), (KCOLS,)),
        )
        if early is not None:
            self.early.add_steps(steps, KT, EARLY_ORDER, early, ((KOWN,),))
        return steps

    def run(self, order, own, place_own, prepare, early):
        steps = self.steps(own, place_own, prepare, early)
        names = list(steps)
        done = set()
        for number in order:
            name = names[number]
            assert set(steps[name].before) <= done and name not in done, name
            steps[name].run(self.wires)
            done.add(name)
        assert len(done) == len(steps)
        return self.reduction.result, self.small.result


def whole_kernel(total_rows, table, tiles, block, image_x, image_w, grams, *scratch):
    (stage, stage_sems, pairs, sums, resid, early_slots, send_sems, recv_sems), scratch = (
        scratch[:8],
        scratch[8:],
    )
    sets = scratch[: len(scratch) // 2], scratch[len(scratch) // 2 :]
    place = Place()
    K, width = block.shape
    T = width // 2
    count = tiles.shape[0]
    depth = stage.shape[0]

    def fetch(s, slot):
        return pltpu.make_async_copy(tiles.at[s], stage.at[slot], stage_sems.at[slot])

    for s in range(depth):
        fetch(s, s).start()
    greet(near_peers(place) + sum_peers(place))
    wires = Wires(place, send_sems, recv_sems)

    def split_tiles(start, stop, more):
        def step(s, carry):
            slot = lax.rem(s, depth)
            fetch(s, slot).wait()
            pairs[s, 0], pairs[s, 1] = split(stage[slot])
            if more:
                fetch(s + depth, slot).start()
            return carry

        lax.fori_loop(start, stop, step, 0)

    prepare = [
        functools.partial(split_tiles, start, start + PREPARE, start + PREPARE + depth <= count)
        for start in range(0, count, PREPARE)
    ]

    def apply(number):
        near, far, part_rows, part_cols, slots, *boxes = sets[number]
        return Application(
            place, wires, table, pairs, sums, near, far, part_rows, part_cols, boxes, slots, early_slots
        )

    sums[0] = jnp.zeros((K, T), F32)
    first = apply(0)

    def place_block():
        for u in range(2):
            half = block[:, u * T : (u + 1) * T]
            first.near[place.col * 2 + u] = half
            first.far[place.row * 2 + u] = half

    halves, total = first.run(
        FIRST_ORDER,
        lambda u: block.at[:, pl.ds(u * T, T)], place_block, prepare, None
    )
    mean = unfold(total) / total_rows
    for u in range(2):
        resid[u] = halves[u] - dot_n(mean, block[:, u * T : (u + 1) * T], HIGHEST)
    second = apply(1)
    local = {}

    def place_resid():
        grams[0] = mean
        cross = jnp.zeros((K, K), F32)
        square = jnp.zeros((K, K), F32)
        for u in range(2):
            image_x[:, u * T : (u + 1) * T] = halves[u]
            value = resid[u]
            second.near[place.col * 2 + u] = value
            second.far[place.row * 2 + u] = value
            cross += dot_t(halves[u], value, HIGHEST)
            square += dot_t(value, value, HIGHEST)
        grams[1] = cross
        grams[3] = square

    def early():
        return jnp.concatenate([fold(grams[1]), fold(grams[3])], axis=0)

    halves, total = second.run(
        SECOND_ORDER, lambda u: resid.at[u], place_resid, (), early
    )
    for u in range(2):
        image_w[:, u * T : (u + 1) * T] = halves[u]
    half = K // 2
    grams[1] = unfold(second.early.result[:half]) / total_rows
    grams[2] = unfold(total) / total_rows
    grams[3] = unfold(second.early.result[half:]) / total_rows
    wires.drain()


def table_kernel(count, row_ids, col_ids, table):
    live = count[0]
    slots = row_ids.shape[0]

    def clear(s, carry):
        for line in range(2, 6):
            table[line, s] = 0
        return carry

    lax.fori_loop(0, slots, clear, 0)

    def step(s, carry):
        row, col = row_ids[s], col_ids[s]
        table[0, s] = row
        table[1, s] = col
        alive = s < live
        for line, at in ((4, row), (5, col)):
            before = table[line, at]
            table[line - 2, s] = jnp.where(alive, before, 0)
            table[line, at] = jnp.where(alive, s + 1, before)
        return carry

    lax.fori_loop(0, slots, step, 0)


def hand_over(*refs):
    half = len(refs) // 2
    for source, target in zip(refs[:half], refs[half:]):
        target[...] = source[...]


def vmem(count):
    return [pl.BlockSpec(memory_space=pltpu.VMEM)] * count


def on_device(tile_count, tile_rows, tile_cols, tiles, block):
    K, width = block.shape
    T = tiles.shape[-1]
    slots = tiles.shape[2]
    total_rows = width * lax.axis_size("row") * lax.axis_size("col")
    smem = pl.BlockSpec(memory_space=pltpu.SMEM)
    table = pl.pallas_call(
        table_kernel,
        out_shape=jax.ShapeDtypeStruct((6, slots), jnp.int32),
        in_specs=[smem] * 3,
        out_specs=smem,
        name="slot_table",
    )(tile_count[0], tile_rows[0, 0], tile_cols[0, 0])
    strip = pltpu.VMEM((32, K, T), F32)
    seg = jax.ShapeDtypeStruct((K, width), F32)

    one_set = [strip] * 4 + [pltpu.VMEM((5, 4, K // 2, 2 * K), F32)] + reduce_scratch(K, T)

    shapes = (seg, seg, jax.ShapeDtypeStruct((4, K, K), F32))
    results = pl.pallas_call(
        functools.partial(whole_kernel, total_rows),
        out_shape=shapes,
        in_specs=[smem, pl.BlockSpec(memory_space=pl.ANY)] + vmem(1),
        out_specs=tuple(vmem(3)),
        scratch_shapes=[
            pltpu.VMEM((STAGE, T, T), F32),
            pltpu.SemaphoreType.DMA((STAGE,)),
            pltpu.VMEM((slots, 2, T, T), BF16),
            pltpu.VMEM((slots + 1, K, T), F32),
            pltpu.VMEM((2, K, T), F32),
            pltpu.VMEM((5, 4, K, 2 * K), F32),
            pltpu.SemaphoreType.DMA((300,)),
            pltpu.SemaphoreType.DMA((300,)),
        ]
        + one_set * 2,
        compiler_params=pltpu.CompilerParams(
            collective_id=0, has_side_effects=True, vmem_limit_bytes=VMEM_LIMIT
        ),
        name="rayleigh_ritz",
    )(table, tiles[0, 0], block)
    return pl.pallas_call(
        hand_over,
        out_shape=shapes,
        in_specs=vmem(3),
        out_specs=tuple(vmem(3)),
        name="hand_over",
    )(*results)


def solution(mesh):
    return jax.shard_map(
        on_device,
        mesh=mesh,
        in_specs=(
            P("row", "col"),
            P("row", "col", None),
            P("row", "col", None),
            P("row", "col", None, None, None),
            P(None, ("row", "col")),
        ),
        out_specs=(P(None, ("row", "col")), P(None, ("row", "col")), P()),
        check_vma=False,
    )
```

time: 152 us -> 115 us (0.76)
  Pallas kernels: 146 us -> 113 us
  local copies, waits for them, and re-layouts: 4.7 us -> 0 us
    pallas_call x1 -> x2, Pallas kernels: 144 us -> 111 us  [the longest x1 109 us: on_device(): pl.pallas_call(functools.partial(whole_kernel, total_rows), out_shape=sha...]
    unnamed x3 -> x0, local copies, waits for them, and re-layouts: 4.7 us -> none
where the time goes in v3:
time: 115 us; the launch traced here: 114 us
  Pallas kernels  113 us (98%)
  between operations  1.29 us (1%)
    pallas_call x1, Pallas kernels, on_device(): pl.pallas_call(functools.partial(whole_kernel, total_rows), out_shape=sha...  109 us

profile of v3, /device:TPU:1, one launch (start us, length us, event | category | flops | bytes accessed | tf_op | source)
XLA Modules:
  0.0 114.2 jit_solution(5783807396726198599)
XLA Ops:
  1.3 2.2 %slot_table.1.table = s32[6,40]{1,0:T(8,128)} custom-call(s32[1]{0:T(128)} %bitcast.4.count, s32[40]{0:T(128)} %bitcast.6, s32[40]{0:T(128)} %bitcast.7), custom_call_target="tpu_custom_call" | custom-call | tf_op jit(solution)/shard_map/slot_table/pallas_call | solution.py:833
  3.5 109.0 %rayleigh_ritz.1 = (f32[64,512]{1,0:T(8,128)}, f32[64,512]{1,0:T(8,128)}, f32[4,64,64]{2,1,0:T(8,128)}) custom-call(s32[6,40]{1,0:T(8,128)} %slot_table.1.table, f32[40,256,256]{2,1,0:T(8,128)} %bitcast.5, f32[64,512]{1,0:T(8,128)} %block.1), custom_call_target="tpu_custom_call" | custom-call | tf_op jit(solution)/shard_map/rayleigh_ritz/pallas_call | solution.py:846
  112.4 1.8 %hand_over.1 = (f32[64,512]{1,0:T(8,128)}, f32[64,512]{1,0:T(8,128)}, f32[4,64,64]{2,1,0:T(8,128)}) custom-call(f32[64,512]{1,0:T(8,128)} %get-tuple-element.6.refs_0_, f32[64,512]{1,0:T(8,128)} %get-tuple-element.7.refs_1_, f32[4,64,64]{2,1,0:T(8,128)} %get-tuple-element.8.refs_2_), custom_call_target="tpu_custom_call" | custom-call | tf_op jit(solution)/shard_map/hand_over/pallas_call | solution.py:867

commit v4 on v3

--- a/solution.py
+++ b/solution.py
@@ -15,7 +15,7 @@
 VMEM_LIMIT = 60 * 1024 * 1024
 UNROLL = 8
 CHUNKS = 5
-PREPARE = 4
+PREPARE = 2
 STAGE = 16
 (
     KSTART, KOWN, KZL, KZP, KZM, KZO, KXA, KXB, KYP, KYM, KYO, KNEAR, KFAR, KP, KU, KCOLS, KL,
@@ -34,18 +34,19 @@
 SUM_ORDER = (0, 4, 1, 3, 2)
 EARLY_ORDER = (3, 1, 4, 2, 0)
 FIRST_ORDER = (
-    0, 31, 32, 33, 34, 9, 17, 18, 35, 36, 10, 2, 20, 21, 7, 1, 37, 19, 5, 38, 3, 39, 11, 22, 40, 6, 23, 24, 41,
-    14, 8, 26, 27, 13, 4, 25, 12, 28, 29, 16, 42, 43, 44, 15, 45, 46, 47, 54, 55, 63, 70, 56, 57, 62, 71, 30,
-    48, 119, 58, 74, 59, 67, 49, 64, 120, 73, 50, 51, 65, 72, 52, 66, 53, 86, 75, 60, 111, 61, 112, 87, 91, 80,
-    99, 81, 92, 88, 93, 100, 89, 78, 101, 79, 121, 69, 113, 90, 94, 102, 76, 114, 103, 104, 95, 96, 68, 77, 122,
-    115, 105, 116, 106, 107, 82, 83, 108, 97, 98, 123, 109, 84, 85, 110, 117, 124, 118,
+    0, 31, 32, 33, 34, 35, 36, 37, 9, 17, 18, 38, 39, 40, 10, 20, 21, 2, 7, 41, 1, 42, 43, 5, 19, 44, 3, 45, 46,
+    22, 11, 47, 48, 23, 24, 49, 6, 50, 8, 14, 26, 27, 13, 51, 4, 25, 12, 28, 16, 29, 52, 53, 54, 15, 55, 56, 57,
+    64, 65, 73, 80, 66, 67, 72, 81, 30, 58, 129, 68, 69, 77, 84, 59, 74, 83, 130, 60, 61, 75, 82, 62, 63, 96,
+    76, 85, 70, 121, 71, 122, 97, 101, 109, 88, 89, 102, 98, 103, 110, 99, 111, 90, 91, 131, 100, 79, 123, 112,
+    104, 86, 124, 113, 114, 105, 106, 78, 87, 132, 125, 115, 126, 116, 92, 93, 117, 118, 107, 133, 108, 94, 95,
+    119, 120, 127, 134, 128,
 )
 SECOND_ORDER = (
-    0, 31, 115, 9, 17, 18, 10, 20, 21, 2, 7, 1, 116, 19, 5, 3, 22, 11, 23, 24, 6, 26, 14, 8, 27, 13, 117, 4, 25,
-    12, 28, 29, 32, 16, 33, 34, 15, 35, 36, 37, 44, 45, 53, 60, 118, 46, 47, 52, 61, 30, 38, 109, 48, 64, 49,
-    57, 39, 54, 110, 63, 40, 41, 55, 62, 42, 56, 43, 76, 65, 119, 50, 101, 51, 102, 77, 81, 70, 89, 71, 82, 78,
-    83, 90, 79, 68, 91, 69, 111, 59, 103, 80, 84, 92, 66, 104, 93, 120, 94, 85, 86, 58, 67, 112, 105, 95, 106,
-    96, 97, 72, 73, 98, 87, 88, 113, 99, 74, 75, 100, 107, 114, 108,
+    0, 31, 115, 9, 17, 18, 10, 20, 21, 2, 7, 1, 116, 5, 19, 3, 22, 11, 23, 24, 6, 26, 14, 8, 27, 13, 117, 4, 25,
+    12, 28, 29, 32, 16, 33, 34, 15, 35, 36, 37, 44, 45, 53, 60, 118, 46, 47, 52, 61, 30, 38, 109, 48, 49, 57,
+    64, 39, 54, 63, 110, 40, 41, 55, 62, 42, 43, 76, 56, 65, 119, 50, 101, 51, 102, 77, 81, 89, 68, 69, 82, 78,
+    83, 90, 79, 91, 70, 71, 111, 80, 59, 103, 92, 120, 84, 66, 104, 93, 94, 85, 86, 58, 67, 112, 105, 95, 106,
+    96, 72, 73, 97, 98, 87, 113, 88, 74, 75, 99, 100, 107, 114, 108,
 )
 
 
@@ -699,7 +700,10 @@
         return self.reduction.result, self.small.result
 
 
-def whole_kernel(total_rows, table, tiles, block, image_x, image_w, grams, *scratch):
+def whole_kernel(
+    total_rows, live, row_ids, col_ids, row_line, col_line, tiles, block, image_x, image_w, grams, *scratch
+):
+    lines, table, table_sem, *scratch = scratch
     (stage, stage_sems, pairs, sums, resid, early_slots, send_sems, recv_sems), scratch = (
         scratch[:8],
         scratch[8:],
@@ -716,7 +720,11 @@
 
     for s in range(depth):
         fetch(s, s).start()
+    fill_lines(live[0], row_ids, col_ids, row_line, col_line, lines)
+    to_scalars = pltpu.make_async_copy(lines, table, table_sem)
+    to_scalars.start()
     greet(near_peers(place) + sum_peers(place))
+    to_scalars.wait()
     wires = Wires(place, send_sems, recv_sems)
 
     def split_tiles(start, stop, more):
@@ -789,29 +797,30 @@
     wires.drain()
 
 
-def table_kernel(count, row_ids, col_ids, table):
-    live = count[0]
-    slots = row_ids.shape[0]
-
-    def clear(s, carry):
-        for line in range(2, 6):
-            table[line, s] = 0
-        return carry
-
-    lax.fori_loop(0, slots, clear, 0)
-
-    def step(s, carry):
-        row, col = row_ids[s], col_ids[s]
-        table[0, s] = row
-        table[1, s] = col
-        alive = s < live
-        for line, at in ((4, row), (5, col)):
-            before = table[line, at]
-            table[line - 2, s] = jnp.where(alive, before, 0)
-            table[line, at] = jnp.where(alive, s + 1, before)
-        return carry
-
-    lax.fori_loop(0, slots, step, 0)
+def fill_lines(live, row_ids, col_ids, row_line, col_line, lines):
+    slots = row_line.shape[1]
+    lane = lax.broadcasted_iota(jnp.int32, row_line.shape, 1)
+    rows, cols = row_line[...], col_line[...]
+    none = jnp.zeros_like(rows)
+
+    def step(t, carry):
+        before_row, before_col, last_row, last_col = carry
+        alive = t < live
+        row = jnp.where(alive, row_ids[t], -1)
+        col = jnp.where(alive, col_ids[t], -1)
+        later = lane > t
+        number = t + 1
+        return (
+            jnp.where(jnp.logical_and(rows == row, later), number, before_row),
+            jnp.where(jnp.logical_and(cols == col, later), number, before_col),
+            jnp.where(lane == row, number, last_row),
+            jnp.where(lane == col, number, last_col),
+        )
+
+    lines[...] = jnp.zeros_like(lines)
+    found = lax.fori_loop(0, slots, step, (none, none, none, none))
+    for line, value in enumerate((rows, cols) + found):
+        lines[line : line + 1, :slots] = value
 
 
 def hand_over(*refs):
@@ -830,13 +839,6 @@
     slots = tiles.shape[2]
     total_rows = width * lax.axis_size("row") * lax.axis_size("col")
     smem = pl.BlockSpec(memory_space=pltpu.SMEM)
-    table = pl.pallas_call(
-        table_kernel,
-        out_shape=jax.ShapeDtypeStruct((6, slots), jnp.int32),
-        in_specs=[smem] * 3,
-        out_specs=smem,
-        name="slot_table",
-    )(tile_count[0], tile_rows[0, 0], tile_cols[0, 0])
     strip = pltpu.VMEM((32, K, T), F32)
     seg = jax.ShapeDtypeStruct((K, width), F32)
 
@@ -846,9 +848,12 @@
     results = pl.pallas_call(
         functools.partial(whole_kernel, total_rows),
         out_shape=shapes,
-        in_specs=[smem, pl.BlockSpec(memory_space=pl.ANY)] + vmem(1),
+        in_specs=[smem] * 3 + vmem(2) + [pl.BlockSpec(memory_space=pl.ANY)] + vmem(1),
         out_specs=tuple(vmem(3)),
         scratch_shapes=[
+            pltpu.VMEM((8, 128), jnp.int32),
+            pltpu.SMEM((8, 128), jnp.int32),
+            pltpu.SemaphoreType.DMA,
             pltpu.VMEM((STAGE, T, T), F32),
             pltpu.SemaphoreType.DMA((STAGE,)),
             pltpu.VMEM((slots, 2, T, T), BF16),
@@ -863,7 +868,15 @@
             collective_id=0, has_side_effects=True, vmem_limit_bytes=VMEM_LIMIT
         ),
         name="rayleigh_ritz",
-    )(table, tiles[0, 0], block)
+    )(
+        tile_count[0],
+        tile_rows[0, 0],
+        tile_cols[0, 0],
+        tile_rows[0],
+        tile_cols[0],
+        tiles[0, 0],
+        block,
+    )
     return pl.pallas_call(
         hand_over,
         out_shape=shapes,

time: 115 us -> 113 us (0.983)
    pallas_call x1 -> x0, Pallas kernels: 2.18 us -> none  [on_device(): pl.pallas_call(table_kernel, out_shape=jax.ShapeDtypeStruct((6, slots), j...]
where the time goes in v4:
time: 113 us
  Pallas kernels  112 us (99%)
  between operations  1.28 us (1%)
    pallas_call x1, Pallas kernels, on_device(): pl.pallas_call(functools.partial(whole_kernel, total_rows), out_shape=sha...  110 us

profile of v4, /device:TPU:1, one launch (start us, length us, event | category | flops | bytes accessed | tf_op | source)
XLA Modules:
  0.0 113.2 jit_solution(11609746530175488327)
XLA Ops:
  1.3 110.1 %rayleigh_ritz.1 = (f32[64,512]{1,0:T(8,128)}, f32[64,512]{1,0:T(8,128)}, f32[4,64,64]{2,1,0:T(8,128)}) custom-call(s32[1]{0:T(128)} %bitcast.6.live, s32[40]{0:T(128)} %bitcast.8, s32[40]{0:T(128)} %bitcast.10, s32[1,40]{1,0:T(1,128)} %bitcast.9, s32[1,40]{1,0:T(1,128)} %bitcast.11, f32[40,256,256]{2,1,0:T(8,128)} %bitcast.7, f32[64,512]{1,0:T(8,128)} %block.1), custom_call_target="tpu_custom_call" | custom-call | tf_op jit(solution)/shard_map/rayleigh_ritz/pallas_call | solution.py:848
  111.4 1.8 %hand_over.1 = (f32[64,512]{1,0:T(8,128)}, f32[64,512]{1,0:T(8,128)}, f32[4,64,64]{2,1,0:T(8,128)}) custom-call(f32[64,512]{1,0:T(8,128)} %get-tuple-element.6.refs_0_, f32[64,512]{1,0:T(8,128)} %get-tuple-element.7.refs_1_, f32[4,64,64]{2,1,0:T(8,128)} %get-tuple-element.8.refs_2_), custom_call_target="tpu_custom_call" | custom-call | tf_op jit(solution)/shard_map/hand_over/pallas_call | solution.py:880
